TPU v7x, 128 devices: a whole 4x4x4 slice. The times are simulated.
128 devices in a mesh: row: 64 (over z, y, x), col: 2 (over core).
Axes of the slice: x: 4, y: 4, z: 4, core: 2. Of those that a mesh axis runs over, the one named last changes fastest.
Arguments:
- gate_weight: bfloat16 [8192, 29568], P('row', 'col'), may hold values from -800 to 800
- up_weight: bfloat16 [8192, 29568], P('row', 'col'), may hold values from -800 to 800
- down_weight: bfloat16 [29568, 8192], P('row', 'col'), may hold values from -800 to 800
- gate_in: bfloat16 [8192, 64], P(('row', 'col')), may hold values from -6 to 6
- gate_out: bfloat16 [64, 29568], P(None, 'col'), may hold values from -3 to 3
- up_in: bfloat16 [8192, 64], P(('row', 'col')), may hold values from -6 to 6
- up_out: bfloat16 [64, 29568], P(None, 'col'), may hold values from -3 to 3
- down_in: bfloat16 [29568, 64], P(('row', 'col')), may hold values from -6 to 6
- down_out: bfloat16 [64, 8192], P(None, 'col'), may hold values from -3 to 3
- gate_magnitude: float32 [29568], P('col'), may hold values from 20 to 400
- up_magnitude: float32 [29568], P('col'), may hold values from 20 to 400
- down_magnitude: float32 [8192], P('col'), may hold values from 20 to 400
Outputs:
- gate_merged: bfloat16 [8192, 29568], P(None, ('col', 'row'))
- up_merged: bfloat16 [8192, 29568], P(None, ('col', 'row'))
- down_merged: bfloat16 [29568, 8192], P(None, ('col', 'row'))
All inputs are finite; a program needn't handle non-finite values.
Results may differ from a plain program's by a relative error of at most 0.0029.
Values may be sent and summed in bfloat16 or wider, within the bound.
A program may use at most 192 MiB of HBM per device.

v0:
```python
import jax
import jax.numpy as jnp
from jax import lax
from jax.sharding import PartitionSpec as P

epsilon = 1e-06


def side_by_side(arrays, axis, dim, along):
    ends, at = ([], 0)
    for a in arrays[:-1]:
        at += a.shape[along]
        ends.append(at)
    both = jnp.concatenate(arrays, axis=along)
    return tuple(jnp.split(lax.all_gather(both, axis, axis=dim, tiled=True), ends, axis=along))


def combine_update(weight, factor_rows, factor_cols):
    update = jnp.dot(factor_rows, factor_cols, preferred_element_type=jnp.float32)
    return weight.astype(jnp.float32) + update


def column_squares(combined):
    return jnp.sum(combined * combined, axis=0)


def rescale(combined, squares, magnitude):
    column_scale = magnitude / jnp.sqrt(squares + epsilon)
    return (combined * column_scale[None, :]).astype(jnp.bfloat16)


def local(
    gate_weight,
    up_weight,
    down_weight,
    gate_in,
    gate_out,
    up_in,
    up_out,
    down_in,
    down_out,
    gate_magnitude,
    up_magnitude,
    down_magnitude,
):
    outers = (gate_out, up_out, down_out)
    magnitudes = (gate_magnitude, up_magnitude, down_magnitude)
    whole_in = (
        *side_by_side((gate_in, up_in), ("row", "col"), 0, 1),
        lax.all_gather(down_in, ("row", "col"), axis=0, tiled=True),
    )
    position = lax.axis_index("row")
    moved = (
        lax.all_to_all(gate_weight, "row", split_axis=1, concat_axis=0, tiled=True),
        lax.all_to_all(up_weight, "row", split_axis=1, concat_axis=0, tiled=True),
        lax.all_to_all(down_weight, "row", split_axis=1, concat_axis=0, tiled=True),
    )
    results = []
    for which in range(3):
        slab_width = moved[which].shape[1]
        slab_cols = lax.dynamic_slice_in_dim(outers[which], position * slab_width, slab_width, 1)
        slab_mags = lax.dynamic_slice_in_dim(
            magnitudes[which], position * slab_width, slab_width, 0
        )
        combined = combine_update(moved[which], whole_in[which], slab_cols)
        results.append(rescale(combined, column_squares(combined), slab_mags))
    return tuple(results)


def solution(mesh):
    placed = (
        P("row", "col"),
        P("row", "col"),
        P("row", "col"),
        P(("row", "col"), None),
        P(None, "col"),
        P(("row", "col"), None),
        P(None, "col"),
        P(("row", "col"), None),
        P(None, "col"),
        P("col"),
        P("col"),
        P("col"),
    )
    return jax.shard_map(
        local,
        mesh=mesh,
        in_specs=placed,
        out_specs=(P(None, ("col", "row")), P(None, ("col", "row")), P(None, ("col", "row"))),
        check_vma=False,
    )
```

profile of v0, /device:TPU:1, one launch (start us, length us, event | category | flops | bytes accessed | tf_op | source)
XLA Modules:
  0.0 312.3 jit_solution(16435701961778984731)
XLA Ops:
  7.2 5.0 %all_to_all.32 = bf16[128,64,231]{0,2,1:T(8,128)(2,1)} reshape(bf16[128,14784]{0,1:T(8,128)(2,1)} %param.13) | data formatting | bytes 7569408 | tf_op jit(solution)/shard_map/all_to_all | solution.py:55
  12.2 12.2 %all-to-all-start.1 = ((bf16[128,64,231]{0,2,1:T(8,128)(2,1)}), bf16[128,64,231]{0,2,1:T(8,128)(2,1)}, u32[]{:S(2)}, u32[]{:S(2)}) async-start(bf16[128,64,231]{0,2,1:T(8,128)(2,1)} %all_to_all.32), calls=%async_computation.1 | async-start | bytes 7602176 | tf_op jit(solution)/shard_map/all_to_all | solution.py:55
  24.4 4.9 %all_to_all.30 = bf16[128,64,231]{0,2,1:T(8,128)(2,1)} reshape(bf16[128,14784]{0,1:T(8,128)(2,1)} %param.12) | data formatting | bytes 7569408 | tf_op jit(solution)/shard_map/all_to_all | solution.py:54
  29.3 42.9 %all-to-all-done.1 = bf16[128,64,231]{0,2,1:T(8,128)(2,1)} async-done(((bf16[128,64,231]{0,2,1:T(8,128)(2,1)}), bf16[128,64,231]{0,2,1:T(8,128)(2,1)}, u32[]{:S(2)}, u32[]{:S(2)}) %all-to-all-start.1) | async-done | bytes 3784736 | tf_op jit(solution)/shard_map/all_to_all | solution.py:55
  72.3 9.1 %all-to-all-start = ((bf16[128,64,231]{0,2,1:T(8,128)(2,1)}), bf16[128,64,231]{0,2,1:T(8,128)(2,1)}, u32[]{:S(2)}, u32[]{:S(2)}) async-start(bf16[128,64,231]{0,2,1:T(8,128)(2,1)} %all_to_all.30), calls=%async_computation | async-start | bytes 7602176 | tf_op jit(solution)/shard_map/all_to_all | solution.py:54
  82.1 6.4 %copy.25 = bf16[462,4096]{0,1:T(8,128)(2,1)} copy(bf16[462,4096]{1,0:T(8,128)(2,1)} %param.14) | data formatting | bytes 7569408 | tf_op args[2]
  88.6 39.6 %all-to-all-done = bf16[128,64,231]{0,2,1:T(8,128)(2,1)} async-done(((bf16[128,64,231]{0,2,1:T(8,128)(2,1)}), bf16[128,64,231]{0,2,1:T(8,128)(2,1)}, u32[]{:S(2)}, u32[]{:S(2)}) %all-to-all-start) | async-done | bytes 3784736 | tf_op jit(solution)/shard_map/all_to_all | solution.py:54
  128.1 10.0 %all-to-all-start.2 = ((bf16[462,64,64]{0,2,1:T(8,128)(2,1)}), bf16[462,64,64]{0,2,1:T(8,128)(2,1)}, u32[]{:S(2)}, u32[]{:S(2)}) async-start(bf16[462,64,64]{0,2,1:T(8,128)(2,1)} %bitcast.41), calls=%async_computation.2 | async-start | bytes 8388608 | tf_op jit(solution)/shard_map/all_to_all | solution.py:56
  138.9 2.6 convert_bitcast_fusion.1
  144.4 9.9 %copy.29 = f32[29,8,64,128]{3,1,2,0:T(8,128)} copy(f32[29,8,64,128]{3,2,1,0:T(8,128)S(1)} %bitcast.36) | data formatting | bytes 15204352
  154.3 2.6 convert_bitcast_fusion.2
  160.2 9.9 %copy.28 = f32[29,8,64,128]{3,1,2,0:T(8,128)} copy(f32[29,8,64,128]{3,2,1,0:T(8,128)S(1)} %bitcast.35) | data formatting | bytes 15204352
  170.1 21.4 %all-to-all-done.2 = bf16[462,64,64]{0,2,1:T(8,128)(2,1)} async-done(((bf16[462,64,64]{0,2,1:T(8,128)(2,1)}), bf16[462,64,64]{0,2,1:T(8,128)(2,1)}, u32[]{:S(2)}, u32[]{:S(2)}) %all-to-all-start.2) | async-done | bytes 3784736 | tf_op jit(solution)/shard_map/all_to_all | solution.py:56
  191.6 3.4 %convert_bitcast_fusion = f32[64,462,64]{1,2,0:T(8,128)S(1)} fusion(bf16[462,64,64]{0,2,1:T(8,128)(2,1)} %all-to-all-done.2), kind=kLoop, calls=%fused_computation.4 | loop fusion | flops 1892352 | bytes 11354112 | tf_op jit(solution)/shard_map/convert_element_type | solution.py:20
  195.0 8.2 %copy.26 = f32[64,462,64]{1,0,2:T(8,128)} copy(f32[64,462,64]{1,2,0:T(8,128)S(1)} %convert_bitcast_fusion) | data formatting | bytes 15138816 | tf_op jit(solution)/shard_map/convert_element_type | solution.py:20
  203.2 9.1 %reshape.26 = f32[29568,64]{0,1:T(8,128)} reshape(f32[64,462,64]{1,0,2:T(8,128)} %copy.26) | data formatting | bytes 15138816 | tf_op jit(solution)/shard_map/convert_element_type | solution.py:20
  214.6 5.7 %multiply_reduce_fusion = (f32[231]{0:T(256)S(1)}, f32[8192,231]{0,1:T(8,128)S(1)}) fusion(f32[8192,231]{0,1:T(8,128)} %bitcast.37, bf16[64,14784]{1,0:T(8,128)(2,1)S(1)} %copy-done, s32[]{:T(128)S(6)} %select_n.4, bf16[8192,128]{1,0:T(8,128)(2,1)} %all-gather.4.cloned.1.call-done), kind=kOutput, calls=%fused_computation.8 | convolution fusion | flops 247897888 | bytes 17269664 | tf_op jit(solution)/shard_map/dot_general | solution.py:19
  220.4 4.6 %multiply_reduce_fusion.1 = (f32[231]{0:T(256)S(1)}, f32[8192,231]{0,1:T(8,128)S(1)}) fusion(f32[8192,231]{0,1:T(8,128)} %bitcast.38, bf16[64,14784]{1,0:T(8,128)(2,1)} %param.16, s32[]{:T(128)S(6)} %select_n.4, bf16[8192,128]{1,0:T(8,128)(2,1)S(1)} %copy-done.1), kind=kOutput, calls=%fused_computation.10 | convolution fusion | flops 247897888 | bytes 17302432 | tf_op jit(solution)/shard_map/dot_general | solution.py:19
  225.7 2.6 multiply_convert_fusion
  228.4 2.6 multiply_convert_fusion.1
  230.9 50.8 %all-gather.6.cloned.1.call-done = bf16[128,231,64]{1,2,0:T(8,128)(2,1)} async-done(((bf16[1,231,64]{1,2,0:T(8,128)(2,1)}), bf16[128,231,64]{1,2,0:T(8,128)(2,1)}) %all-gather.6.cloned.1.call-update) | async-done | bytes 3784720 | tf_op jit(solution)/shard_map/all_gather | solution.py:50
  281.7 6.5 %copy.27 = bf16[128,231,64]{1,0,2:T(8,128)(2,1)} copy(bf16[128,231,64]{1,2,0:T(8,128)(2,1)} %all-gather.6.cloned.1.call-done) | data formatting | bytes 7569408 | tf_op jit(solution)/shard_map/all_gather | solution.py:50
  288.3 8.2 %reshape.28 = bf16[29568,64]{0,1:T(8,128)(2,1)} reshape(bf16[128,231,64]{1,0,2:T(8,128)(2,1)} %copy.27) | data formatting | bytes 7569408
  296.5 5.7 %multiply_reduce_fusion.2 = (f32[64]{0:T(128)S(1)}, f32[29568,64]{0,1:T(8,128)S(1)}) fusion(f32[29568,64]{0,1:T(8,128)} %reshape.26, bf16[29568,64]{0,1:T(8,128)(2,1)} %reshape.28, bf16[64,4096]{1,0:T(8,128)(2,1)} %param.20, s32[]{:T(128)S(6)} %select_n.5), kind=kOutput, calls=%fused_computation.14 | convolution fusion | flops 247898048 | bytes 18940164 | tf_op jit(solution)/shard_map/dot_general | solution.py:19
  (21 shorter events, 14.0 us)
Async XLA Ops:
  7.2 207.5 %copy-start = (bf16[64,14784]{1,0:T(8,128)(2,1)S(1)}, bf16[64,14784]{1,0:T(8,128)(2,1)}, u32[]{:S(2)}) copy-start(bf16[64,14784]{1,0:T(8,128)(2,1)} %param.18) | copy-start | bytes 5677060
  12.2 60.0 %all-to-all-start.1 = ((bf16[128,64,231]{0,2,1:T(8,128)(2,1)}), bf16[128,64,231]{0,2,1:T(8,128)(2,1)}, u32[]{:S(2)}, u32[]{:S(2)}) async-start(bf16[128,64,231]{0,2,1:T(8,128)(2,1)} %all_to_all.32), calls=%async_computation.1 | async-start | bytes 7602176 | tf_op jit(solution)/shard_map/all_to_all | solution.py:55
  29.3 52.1 %copy-start.2 = (bf16[64,64]{1,0:T(8,128)(2,1)S(1)}, bf16[64,64]{1,0:T(8,128)(2,1)}, u32[]{:S(2)}) copy-start(bf16[64,64]{1,0:T(8,128)(2,1)} %param.17) | copy-start | bytes 24580
  29.3 52.1 %copy-start.3 = (bf16[64,64]{1,0:T(8,128)(2,1)S(1)}, bf16[64,64]{1,0:T(8,128)(2,1)}, u32[]{:S(2)}) copy-start(bf16[64,64]{1,0:T(8,128)(2,1)} %param.15) | copy-start | bytes 24580
  72.3 55.9 %all-to-all-start = ((bf16[128,64,231]{0,2,1:T(8,128)(2,1)}), bf16[128,64,231]{0,2,1:T(8,128)(2,1)}, u32[]{:S(2)}, u32[]{:S(2)}) async-start(bf16[128,64,231]{0,2,1:T(8,128)(2,1)} %all_to_all.30), calls=%async_computation | async-start | bytes 7602176 | tf_op jit(solution)/shard_map/all_to_all | solution.py:54
  81.4 133.3 %all-gather.4.cloned.1.call-start = ((), (), s32[]{:S(2)}) async-start(), calls=%async_computation.3 | async-start | bytes 2113536 | tf_op jit(solution)/shard_map/all_gather | solution.py:15
  128.1 63.4 %all-to-all-start.2 = ((bf16[462,64,64]{0,2,1:T(8,128)(2,1)}), bf16[462,64,64]{0,2,1:T(8,128)(2,1)}, u32[]{:S(2)}, u32[]{:S(2)}) async-start(bf16[462,64,64]{0,2,1:T(8,128)(2,1)} %bitcast.41), calls=%async_computation.2 | async-start | bytes 8388608 | tf_op jit(solution)/shard_map/all_to_all | solution.py:56
  138.1 143.6 %all-gather.6.cloned.1.call-start = ((), (), s32[]{:S(2)}) async-start(), calls=%async_computation.4 | async-start | bytes 4227072 | tf_op jit(solution)/shard_map/all_gather | solution.py:50
  214.6 5.7 %copy-start.1 = (bf16[8192,128]{1,0:T(8,128)(2,1)S(1)}, bf16[8192,128]{1,0:T(8,128)(2,1)}, u32[]{:S(2)}) copy-start(bf16[8192,128]{1,0:T(8,128)(2,1)} %all-gather.4.cloned.1.call-done) | copy-start | bytes 6291460
Sparse Core Ops, SparseCore 0:
  85.9 128.6 all-gather.3
  217.8 63.9 all-gather.5
where the time goes:
time: 317 us; the launch traced here: 312 us
  waiting for transfers between devices  158 us (50%)
  local copies, waits for them, and re-layouts  74.5 us (24%)
  starting transfers between devices  31.5 us (10%)
  other arithmetic  18.4 us (6%)
  matrix products  16 us (5%)
  between operations  14.3 us (5%)
    all_gather x1, waiting for transfers between devices, local(): lax.all_gather(down_in, ('row', 'col'), axis=0, tiled=True)  50.8 us
    all_to_all x1, waiting for transfers between devices, local(): lax.all_to_all(up_weight, 'row', split_axis=1, concat_axis=0, tiled=True)  42.9 us
    all_to_all x1, waiting for transfers between devices, local(): lax.all_to_all(gate_weight, 'row', split_axis=1, concat_axis=0, tiled=True)  39.6 us
    unnamed x14, local copies, waits for them, and re-layouts  37.3 us
    all_to_all x1, waiting for transfers between devices, local(): lax.all_to_all(down_weight, 'row', split_axis=1, concat_axis=0, tiled=True)  21.4 us
    convert_element_type x4, local copies, waits for them, and re-layouts, combine_update(): return weight.astype(jnp.float32) + update  20.7 us
    dot_general x3, matrix products, combine_update(): jnp.dot(factor_rows, factor_cols, preferred_element_type=jnp.float32)  16 us
    all_to_all x1, starting transfers between devices, local(): lax.all_to_all(up_weight, 'row', split_axis=1, concat_axis=0, tiled=True)  12.2 us
  transfers between devices with their start and end apart: 5, of which 5 were waited for; matrix products, arithmetic and copies ran while one was open for 24% of the time, Pallas kernels for 0%

commit v1 on v0

v1 whole, which is shorter than its diff:
```python
import functools

import jax
import jax.numpy as jnp
from jax import lax
from jax.experimental import pallas as pl
from jax.experimental.pallas import tpu as pltpu
from jax.sharding import PartitionSpec as P

MESH = pl.DeviceIdType.MESH
BF = jnp.bfloat16
F32 = jnp.float32
EPS = 1e-06
RANK = 64
N = 64
COLS = 14784
SLAB = 231
DROWS = 462
DCOLS = 4096
WINDOW = 512
BLK = 1024
ORDERS = ((2, 1, 0), (1, 0, 2), (0, 2, 1))
FIRST = (0, 120, 240)
PARTS = ((0, 96), (96, 88), (184, 88))
CHUNKS = (((0, 128), (128, 104)), ((0, 128), (128, 104)), ((0, 32), (32, 32)))


def peer_of(me, axis, k):
    stride = (16, 4, 1)[axis]
    mine = lax.rem(lax.div(me, stride), 4)
    other = lax.rem(mine + k, 4)
    return me + (other - mine) * stride, mine, other


def greet(me, core, partner):
    bar = pltpu.get_barrier_semaphore()
    for axis in range(3):
        for k in (1, 2, 3):
            p, _, _ = peer_of(me, axis, k)
            pl.semaphore_signal(bar, inc=1, device_id=(p, core), device_id_type=MESH)
    if partner:
        pl.semaphore_signal(bar, inc=1, device_id=(me, 1 - core), device_id_type=MESH)
    pl.semaphore_wait(bar, 10 if partner else 9)


def eye(h):
    return lax.broadcasted_iota(jnp.int32, (h, 128), 0) == lax.broadcasted_iota(
        jnp.int32, (h, 128), 1
    )


def to_lanes(x):
    n = x.shape[0]
    sums = jnp.sum(x, axis=1, keepdims=True)
    rows = []
    for b in range(0, n, 128):
        h = min(128, n - b)
        rows.append(jnp.sum(jnp.where(eye(h), sums[b : b + h], 0.0), axis=0, keepdims=True))
    return jnp.concatenate(rows, axis=0)


def to_sublanes(row, h):
    return jnp.sum(jnp.where(eye(h), row, 0.0), axis=1, keepdims=True)


def combined_t(w, q, p, start, n):
    upd = lax.dot_general(
        q[:, pl.ds(start, n)], p, (((0,), (1,)), ((), ())), preferred_element_type=F32
    )
    return w[pl.ds(start, n), :].astype(F32) + upd


def prep_kernel(
    wg, wu, wd, qg, qu, qd, pg, pu, pd, mags,
    og, ou, od,
    vg, vu, vd, sg, su, sd, full, turn, both_g, both_u, both_d, pdown, sums, got, scale,
    in_sem, p_send, p_recv, p_loc, r_send, r_recv, out_sem,
):
    me = lax.axis_index("row")
    core = lax.axis_index("col")
    loads = []
    for i, (src, dst) in enumerate(((wg, vg), (wu, vu), (wd, vd))):
        cp = pltpu.make_async_copy(src, dst, in_sem.at[i])
        cp.start()
        loads.append(cp)
    greet(me, core, True)
    ps = []
    for i, (src, dst) in enumerate(((pg, both_g), (pu, both_u), (pd, both_d))):
        far = pltpu.make_async_remote_copy(
            src_ref=src, dst_ref=dst.at[core], send_sem=p_send.at[i], recv_sem=p_recv.at[i],
            device_id=(me, 1 - core), device_id_type=MESH,
        )
        near = pltpu.make_async_copy(src, dst.at[core], p_loc.at[i])
        far.start()
        near.start()
        ps.append((far, near))
    for far, near in ps:
        near.wait()
        far.wait()

    for i, (w, q, both) in enumerate(((vg, qg, both_g), (vu, qu, both_u))):
        loads[i].wait()
        p = both[...].reshape(2 * RANK, RANK)

        def squares(b, carry, w=w, q=q, p=p, first=FIRST[i]):
            x = combined_t(w, q, p, pl.multiple_of(b * BLK, BLK), BLK)
            sums[0, pl.ds(pl.multiple_of(first + b * 8, 8), 8), :] = to_lanes(x * x)
            return carry

        lax.fori_loop(0, COLS // BLK, squares, 0)
        x = combined_t(w, q, p, COLS // BLK * BLK, COLS % BLK)
        sums[0, FIRST[i] + 112 : FIRST[i] + 116, :] = to_lanes(x * x)
        sums[0, FIRST[i] + 116 : FIRST[i] + 120, :] = jnp.zeros((4, 128), F32)
    pdown[0:231, :] = both_d[0].astype(F32).T
    pdown[231:462, :] = both_d[1].astype(F32).T
    p = pdown[0:DROWS, :].astype(BF)
    loads[2].wait()

    def down_block(j):
        at = pl.ds(pl.multiple_of(j * 128, 128), 128)
        upd = jnp.dot(p, qd[:, at], preferred_element_type=F32)
        return vd[:, at].astype(F32) + upd

    def squares_down(j, carry):
        x = down_block(j)
        sums[0, pl.ds(FIRST[2] + j, 1), :] = jnp.sum(x * x, axis=0, keepdims=True)
        return carry

    lax.fori_loop(0, DCOLS // 128, squares_down, 0)

    def exchange(ph, t):
        res = []
        at = pl.ds(*PARTS[t])
        for k in (2, 1, 3):
            q, _, _ = peer_of(me, ORDERS[t][ph], k)
            res.append(
                pltpu.make_async_remote_copy(
                    src_ref=sums.at[ph, at], dst_ref=got.at[ph, k - 1, at],
                    send_sem=r_send.at[ph, t, k - 1], recv_sem=r_recv.at[ph, t, k - 1],
                    device_id=(q, core), device_id_type=MESH,
                )
            )
        return res

    for t in range(3):
        for cp in exchange(0, t):
            cp.start()
    for ph in range(3):
        for t in range(3):
            for cp in exchange(ph, t):
                cp.wait_recv()
            at = pl.ds(*PARTS[t])
            total = sums[ph, at, :] + got[ph, 0, at, :] + got[ph, 1, at, :] + got[ph, 2, at, :]
            if ph < 2:
                sums[ph + 1, at, :] = total
                for cp in exchange(ph + 1, t):
                    cp.start()
            else:
                scale[at, :] = mags[at, :] / jnp.sqrt(total + EPS)
    for ph in range(3):
        for t in range(3):
            for cp in exchange(ph, t):
                cp.wait_send()

    outs = []
    for i, (w, q, both, s, o) in enumerate(
        ((vg, qg, both_g, sg, og), (vu, qu, both_u, su, ou))
    ):
        p = both[...].reshape(2 * RANK, RANK)

        def merge(b, carry, w=w, q=q, p=p, first=FIRST[i]):
            start = pl.multiple_of(b * BLK, BLK)
            x = combined_t(w, q, p, start, BLK)
            f = scale[pl.ds(pl.multiple_of(first + b * 8, 8), 8), :]
            for e in range(8):
                full[pl.ds(pl.multiple_of(start + e * 128, 128), 128), :] = x[
                    e * 128 : (e + 1) * 128
                ] * to_sublanes(f[e : e + 1], 128)
            return carry

        lax.fori_loop(0, COLS // BLK, merge, 0)
        start = COLS // BLK * BLK
        x = combined_t(w, q, p, start, COLS % BLK)
        f = scale[FIRST[i] + 112 : FIRST[i] + 116, :]
        for e in range(4):
            h = 128 if e < 3 else 64
            full[start + e * 128 : start + e * 128 + h, :] = x[
                e * 128 : e * 128 + h
            ] * to_sublanes(f[e : e + 1], h)
        full[COLS : COLS + 8, :] = jnp.zeros((8, 128), F32)

        def cut(g, carry, s=s):
            base = pl.multiple_of(g * (8 * SLAB), 8)
            for e in range(8):
                s[g * 8 + e] = full[pl.ds(base + e * SLAB, SLAB + 1), :].astype(BF)
            return carry

        lax.fori_loop(0, N // 8, cut, 0)
        cp = pltpu.make_async_copy(s, o, out_sem.at[i])
        cp.start()
        outs.append(cp)

    p = pdown[0:DROWS, :].astype(BF)
    turn[...] = jnp.zeros_like(turn)
    first = WINDOW - lax.rem(me * DROWS, WINDOW)

    def merge_down(j, carry):
        y = down_block(j) * scale[pl.ds(FIRST[2] + j, 1), :]
        turn[0:DROWS, :] = y
        turn[WINDOW : WINDOW + DROWS, :] = y
        z = turn[pl.ds(first, WINDOW), :].T.astype(BF)
        sd[2 * j] = z[0:64]
        sd[2 * j + 1] = z[64:128]
        return carry

    lax.fori_loop(0, DCOLS // 128, merge_down, 0)
    cp = pltpu.make_async_copy(sd, od, out_sem.at[2])
    cp.start()
    outs.append(cp)
    for cp in outs:
        cp.wait()


def prep(wg, wu, wd, qg, qu, qd, pg, pu, pd, mags):
    hbm = pl.BlockSpec(memory_space=pl.ANY)
    vmem = pl.BlockSpec(memory_space=pltpu.VMEM)
    slab = (N, SLAB + 1, 128)
    dslab = (N, 64, WINDOW)
    dma = pltpu.SemaphoreType.DMA
    return pl.pallas_call(
        prep_kernel,
        out_shape=[jax.ShapeDtypeStruct(s, BF) for s in (slab, slab, dslab)],
        in_specs=[hbm] * 3 + [vmem] * 7,
        out_specs=[hbm] * 3,
        scratch_shapes=[
            pltpu.VMEM((COLS, 128), BF), pltpu.VMEM((COLS, 128), BF),
            pltpu.VMEM((DROWS, DCOLS), BF),
            pltpu.VMEM(slab, BF), pltpu.VMEM(slab, BF), pltpu.VMEM(dslab, BF),
            pltpu.VMEM((COLS + 8, 128), F32), pltpu.VMEM((2 * WINDOW, 128), F32),
            pltpu.VMEM((2, 64, 64), BF), pltpu.VMEM((2, 64, 64), BF), pltpu.VMEM((2, 64, 231), BF),
            pltpu.VMEM((464, 64), F32),
            pltpu.VMEM((3, 272, 128), F32), pltpu.VMEM((3, 3, 272, 128), F32),
            pltpu.VMEM((272, 128), F32),
            dma((3,)), dma((3,)), dma((3,)), dma((3,)), dma((3, 3, 3)), dma((3, 3, 3)), dma((3,)),
        ],
        compiler_params=pltpu.CompilerParams(
            collective_id=0, has_side_effects=True, vmem_limit_bytes=60 * 2**20
        ),
        name="prepare",
    )(wg, wu, wd, qg, qu, qd, pg, pu, pd, mags)


def at(ref, axis, idx, chunk):
    ix = [slice(None)] * 3
    ix[axis] = idx
    return ref.at[(*ix, pl.ds(*chunk))]


def exchange_kernel(*refs):
    ins, outs, s1, s2 = refs[0:3], refs[3:6], refs[6:9], refs[9:12]
    send, recv, near = refs[12:15]
    me = lax.axis_index("row")
    core = lax.axis_index("col")
    greet(me, core, False)
    stages = [(ins[m], s1[m], s2[m], outs[m]) for m in range(3)]

    def copies(ph, ch, m):
        axis = ORDERS[m][ph]
        src, dst = stages[m][ph], stages[m][ph + 1]
        chunk = CHUNKS[m][ch]
        res = []
        for k in (2, 1, 3):
            p, mine, other = peer_of(me, axis, k)
            res.append(
                pltpu.make_async_remote_copy(
                    src_ref=at(src, axis, other, chunk), dst_ref=at(dst, axis, mine, chunk),
                    send_sem=send.at[ph, ch, m, k - 1], recv_sem=recv.at[ph, ch, m, k - 1],
                    device_id=(p, core), device_id_type=MESH,
                )
            )
        loc = pltpu.make_async_copy(
            at(src, axis, mine, chunk), at(dst, axis, mine, chunk), near.at[ph, ch, m]
        )
        return res, loc

    def arrived(ph, ch, m):
        res, loc = copies(ph, ch, m)
        for cp in res:
            cp.wait_recv()
        loc.wait()

    for ph in range(3):
        for ch in range(2):
            for m in range(3):
                if ph > 0:
                    arrived(ph - 1, ch, m)
                res, loc = copies(ph, ch, m)
                for cp in res:
                    cp.start()
                loc.start()
    for ch in range(2):
        for m in range(3):
            arrived(2, ch, m)
    for ph in range(3):
        for ch in range(2):
            for m in range(3):
                for cp in copies(ph, ch, m)[0]:
                    cp.wait_send()


def exchange_all(g, u, d):
    arrays = [a.reshape(4, 4, 4, *a.shape[1:]) for a in (g, u, d)]
    hbm = pl.BlockSpec(memory_space=pl.ANY)
    dma = pltpu.SemaphoreType.DMA
    outs = pl.pallas_call(
        exchange_kernel,
        out_shape=[jax.ShapeDtypeStruct(a.shape, BF) for a in arrays],
        in_specs=[hbm] * 3,
        out_specs=[hbm] * 3,
        scratch_shapes=[pltpu.VMEM(a.shape, BF) for a in arrays] * 2
        + [dma((3, 2, 3, 3)), dma((3, 2, 3, 3)), dma((3, 2, 3))],
        compiler_params=pltpu.CompilerParams(
            collective_id=1, has_side_effects=True, vmem_limit_bytes=60 * 2**20
        ),
        name="exchange",
    )(*arrays)
    return [o.reshape(N, *o.shape[3:]) for o in outs]


def join_kernel(x, o):
    for e in range(8):
        o[:, e * 128 : (e + 1) * 128] = x[e, 0:SLAB, :]


def join(x):
    return pl.pallas_call(
        join_kernel,
        grid=(N // 8,),
        out_shape=jax.ShapeDtypeStruct((SLAB, N * 128), BF),
        in_specs=[pl.BlockSpec((8, SLAB + 1, 128), lambda i: (i, 0, 0))],
        out_specs=pl.BlockSpec((SLAB, 1024), lambda i: (0, i)),
        name="join",
    )(x)


TILES = 33


def join_down_kernel(x, o):
    g = pl.program_id(0)

    def tile(i, carry):
        t = g * TILES + i
        s = lax.div(t * 128, DROWS)
        nxt = jnp.minimum(s + 1, N - 1)
        lanes = pl.ds(pl.multiple_of(lax.rem(t, 4) * 128, 128), 128)
        lane = t * 128 + lax.broadcasted_iota(jnp.int32, (64, 128), 1)
        a = x[s, :, lanes]
        b = x[nxt, :, lanes]
        o[:, pl.ds(pl.multiple_of(i * 128, 128), 128)] = jnp.where(lane < (s + 1) * DROWS, a, b)
        return carry

    lax.fori_loop(0, TILES, tile, 0)


def join_down(x):
    return pl.pallas_call(
        join_down_kernel,
        grid=(7,),
        out_shape=jax.ShapeDtypeStruct((64, 29568), BF),
        in_specs=[pl.BlockSpec((N, 64, WINDOW), lambda i: (0, 0, 0))],
        out_specs=pl.BlockSpec((64, TILES * 128), lambda i: (0, i)),
        name="join_down",
    )(x)


def local(wg, wu, wd, pg, qg, pu, qu, pd, qd, mg, mu, md):
    pad = jnp.zeros((15360 - COLS,), F32)
    mags = jnp.concatenate((mg, pad, mu, pad, md)).reshape(272, 128)
    g, u, d = prep(wg.T, wu.T, wd, qg, qu, qd, pg, pu, pd.T, mags)
    g, u, d = exchange_all(g, u, d)
    return join(g).T, join(u).T, join_down(d).T


def solution(mesh):
    placed = (
        P("row", "col"),
        P("row", "col"),
        P("row", "col"),
        P(("row", "col"), None),
        P(None, "col"),
        P(("row", "col"), None),
        P(None, "col"),
        P(("row", "col"), None),
        P(None, "col"),
        P("col"),
        P("col"),
        P("col"),
    )
    return jax.shard_map(
        local,
        mesh=mesh,
        in_specs=placed,
        out_specs=(P(None, ("col", "row")), P(None, ("col", "row")), P(None, ("col", "row"))),
        check_vma=False,
    )
```

time: 317 us -> 222 us (0.70); the launches traced: 312 us -> 222 us
  Pallas kernels: 0 us -> 219 us
  waiting for transfers between devices: 158 us -> 0 us
  local copies, waits for them, and re-layouts: 74.5 us -> 1.59 us
  starting transfers between devices: 31.5 us -> 0 us
  other arithmetic: 18.4 us -> 0 us
  matrix products: 16 us -> 0 us
  between operations: 14.3 us -> 0.65 us
    pallas_call x0 -> x5, Pallas kernels: none -> 219 us  [the longest x1 133 us: exchange_all(): pl.pallas_call(exchange_kernel, out_shape=[jax.ShapeDtypeStruct(a.shape,...]
    all_to_all x3 -> x0, waiting for transfers between devices: 104 us -> none  [the longest x1 42.9 us: local(): lax.all_to_all(up_weight, 'row', split_axis=1, concat_axis=0, tiled=True)]
    all_gather x2 -> x0, waiting for transfers between devices: 53.1 us -> none  [the longest x1 50.8 us: local(): lax.all_gather(down_in, ('row', 'col'), axis=0, tiled=True)]
    unnamed x14 -> x0, local copies, waits for them, and re-layouts: 37.3 us -> none
    all_to_all x3 -> x0, starting transfers between devices: 31.3 us -> none  [the longest x1 12.2 us: local(): lax.all_to_all(up_weight, 'row', split_axis=1, concat_axis=0, tiled=True)]
    convert_element_type x4 -> x0, local copies, waits for them, and re-layouts: 20.7 us -> none  [combine_update(): return weight.astype(jnp.float32) + update]
    convert_element_type x6 -> x0, other arithmetic: 16.2 us -> none  [the longest x3 8.58 us: combine_update(): return weight.astype(jnp.float32) + update]
    dot_general x3 -> x0, matrix products: 16 us -> none  [combine_update(): jnp.dot(factor_rows, factor_cols, preferred_element_type=jnp.float32)]
  transfers between devices with their start and end apart: 5 -> 0, of which waited for: 5 -> 0; matrix products, arithmetic and copies ran while one was open for 24% -> 0% of each run, Pallas kernels for 0% -> 0%
where the time goes in v1:
time: 222 us
  Pallas kernels  219 us (99%)
    pallas_call x1, Pallas kernels, exchange_all(): pl.pallas_call(exchange_kernel, out_shape=[jax.ShapeDtypeStruct(a.shape,...  133 us
    pallas_call x1, Pallas kernels, prep(): pl.pallas_call(prep_kernel, out_shape=[jax.ShapeDtypeStruct(s, BF) for s...  65.6 us
    pallas_call x2, Pallas kernels, join(): pl.pallas_call(join_kernel, grid=(N // 8,), out_shape=jax.ShapeDtypeStruc...  13.5 us
    pallas_call x1, Pallas kernels, join_down(): pl.pallas_call(join_down_kernel, grid=(7,), out_shape=jax.ShapeDtypeStruc...  7.61 us

profile of v1, /device:TPU:1, one launch (start us, length us, event | category | flops | bytes accessed | tf_op | source)
XLA Modules:
  0.0 221.7 jit_solution(8360099799871967654)
XLA Ops:
  0.6 1.6 concatenate.3
  2.2 65.6 %prepare.1 = (bf16[64,232,128]{2,1,0:T(8,128)(2,1)}, bf16[64,232,128]{2,1,0:T(8,128)(2,1)}, bf16[64,64,512]{2,1,0:T(8,128)(2,1)}) custom-call(bf16[14784,128]{1,0:T(8,128)(2,1)} %bitcast.21, bf16[14784,128]{1,0:T(8,128)(2,1)} %bitcast.22, bf16[462,4096]{1,0:T(8,128)(2,1)} %wd.1, bf16[64,14784]{1,0:T(8,128)(2,1)} %qg.1, bf16[64,14784]{1,0:T(8,128)(2,1)} %qu.1, ...), custom_call_target="tpu_custom_call" | custom-call | tf_op jit(solution)/shard_map/prepare/pallas_call | solution.py:230
  67.9 132.7 %exchange.1 = (bf16[4,4,4,232,128]{4,3,2,1,0:T(8,128)(2,1)}, bf16[4,4,4,232,128]{4,3,2,1,0:T(8,128)(2,1)}, bf16[4,4,4,64,512]{4,3,2,1,0:T(8,128)(2,1)}) custom-call(bf16[4,4,4,232,128]{4,3,2,1,0:T(8,128)(2,1)} %bitcast.15, bf16[4,4,4,232,128]{4,3,2,1,0:T(8,128)(2,1)} %bitcast.16, bf16[4,4,4,64,512]{4,3,2,1,0:T(8,128)(2,1)} %bitcast.13), custom_call_target="tpu_custom_call" | custom-call | tf_op jit(solution)/shard_map/exchange/pallas_call | solution.py:315
  200.6 6.8 %join.2 = bf16[231,8192]{1,0:T(8,128)(2,1)} custom-call(bf16[64,232,128]{2,1,0:T(8,128)(2,1)} %bitcast.20), custom_call_target="tpu_custom_call" | custom-call | tf_op jit(solution)/shard_map/join/pallas_call | solution.py:336
  207.3 6.7 %join.3 = bf16[231,8192]{1,0:T(8,128)(2,1)} custom-call(bf16[64,232,128]{2,1,0:T(8,128)(2,1)} %bitcast.19), custom_call_target="tpu_custom_call" | custom-call | tf_op jit(solution)/shard_map/join/pallas_call | solution.py:336
  214.1 7.6 %join_down.1 = bf16[64,29568]{1,0:T(8,128)(2,1)} custom-call(bf16[64,64,512]{2,1,0:T(8,128)(2,1)} %bitcast.14), custom_call_target="tpu_custom_call" | custom-call | tf_op jit(solution)/shard_map/join_down/pallas_call | solution.py:367
  (1 shorter events, 0.0 us)

commit v2 on v0

v2 whole, which is shorter than its diff:
```python
import functools

import jax
import jax.numpy as jnp
from jax import lax
from jax.experimental import pallas as pl
from jax.experimental.pallas import tpu as pltpu
from jax.sharding import PartitionSpec as P

MESH = pl.DeviceIdType.MESH
BF = jnp.bfloat16
F32 = jnp.float32
EPS = 1e-06
RANK = 64
N = 64
COLS = 14784
SLAB = 231
DROWS = 462
DCOLS = 4096
WINDOW = 512
BLK = 1024
ORDERS = ((2, 1, 0), (1, 0, 2), (0, 2, 1))
FIRST = (0, 120, 240)
SUM_ROWS = (
    ((0, 40), (40, 40), (80, 40)),
    ((120, 40), (160, 40), (200, 40)),
    ((240, 8), (248, 8), (256, 16)),
)
GROUPS = (
    (0, ((0, 80), (80, 80), (160, 72))),
    (1, ((0, 80), (80, 80), (160, 72))),
    (2, ((0, 48), (80, 48), (176, 48))),
    (2, ((48, 32), (128, 48), (224, 32))),
)


def peer_of(me, axis, k):
    stride = (16, 4, 1)[axis]
    mine = lax.rem(lax.div(me, stride), 4)
    other = lax.rem(mine + k, 4)
    return me + (other - mine) * stride, mine, other


def greet(me, core):
    bar = pltpu.get_barrier_semaphore()
    for axis in range(3):
        for k in (1, 2, 3):
            p, _, _ = peer_of(me, axis, k)
            pl.semaphore_signal(bar, inc=1, device_id=(p, core), device_id_type=MESH)
    pl.semaphore_signal(bar, inc=1, device_id=(me, 1 - core), device_id_type=MESH)
    pl.semaphore_wait(bar, 10)


def eye(h):
    return lax.broadcasted_iota(jnp.int32, (h, 128), 0) == lax.broadcasted_iota(
        jnp.int32, (h, 128), 1
    )


def to_lanes(x):
    n = x.shape[0]
    sums = jnp.sum(x, axis=1, keepdims=True)
    rows = []
    for b in range(0, n, 128):
        h = min(128, n - b)
        rows.append(jnp.sum(jnp.where(eye(h), sums[b : b + h], 0.0), axis=0, keepdims=True))
    return jnp.concatenate(rows, axis=0)


def to_sublanes(row, h):
    return jnp.sum(jnp.where(eye(h), row, 0.0), axis=1, keepdims=True)


def combined_t(w, q, p, start, n):
    upd = lax.dot_general(
        q[:, pl.ds(start, n)], p, (((0,), (1,)), ((), ())), preferred_element_type=F32
    )
    return w[pl.ds(start, n), :].astype(F32) + upd


def at(ref, axis, idx, rows):
    ix = [slice(None)] * 3
    ix[axis] = idx
    return ref.at[(*ix, pl.ds(*rows))]


def merge_kernel(
    wg, wu, wd, qg, qu, qd, pg, pu, pd, mags,
    og, ou, od, s1g, s1u, s1d,
    vg, vu, vd, rg, ru, rd, sg, su, sd, s2g, s2u, s2d,
    full, turn, both_g, both_u, both_d, pdown, mag, sums, got, scale,
    w_sem, q_sem, p_send, p_recv, p_loc, r_send, r_recv, x_send, x_recv, x_loc,
):
    me = lax.axis_index("row")
    core = lax.axis_index("col")
    half = 7 * BLK
    w_parts = (pl.ds(0, half), pl.ds(half, COLS - half))
    w_load, q_load = [], []
    for i, (src, dst) in enumerate(((qg, rg), (wg, vg), (qu, ru), (wu, vu), (qd, rd), (wd, vd))):
        if i % 2 == 0:
            cp = pltpu.make_async_copy(src, dst, q_sem.at[i // 2])
            cp.start()
            q_load.append(cp)
        elif i < 5:
            cps = [
                pltpu.make_async_copy(src.at[part], dst.at[part], w_sem.at[i // 2, h])
                for h, part in enumerate(w_parts)
            ]
            for cp in cps:
                cp.start()
            w_load.append(cps)
        else:
            cp = pltpu.make_async_copy(src, dst, w_sem.at[2, 0])
            cp.start()
            w_load.append([cp])
    mag_load = pltpu.make_async_copy(mags, mag, q_sem.at[3])
    mag_load.start()
    greet(me, core)
    ps = []
    for i, (src, dst) in enumerate(((pg, both_g), (pu, both_u), (pd, both_d))):
        far = pltpu.make_async_remote_copy(
            src_ref=src, dst_ref=dst.at[core], send_sem=p_send.at[i], recv_sem=p_recv.at[i],
            device_id=(me, 1 - core), device_id_type=MESH,
        )
        near = pltpu.make_async_copy(src, dst.at[core], p_loc.at[i])
        far.start()
        near.start()
        ps.append((far, near))
    for far, near in ps:
        near.wait()
        far.wait()

    def sum_copy(i, ph, t, k):
        q, _, _ = peer_of(me, ORDERS[t][ph], k)
        rows = pl.ds(*SUM_ROWS[i][t])
        return pltpu.make_async_remote_copy(
            src_ref=sums.at[ph, rows], dst_ref=got.at[ph, k - 1, rows],
            send_sem=r_send.at[i, ph, t, k - 1], recv_sem=r_recv.at[i, ph, t, k - 1],
            device_id=(q, core), device_id_type=MESH,
        )

    def send_sums(i, ph):
        for t in range(3):
            for k in (2, 1, 3):
                sum_copy(i, ph, t, k).start()

    def take_sums(i, ph):
        for t in range(3):
            for k in (2, 1, 3):
                sum_copy(i, ph, t, k).wait_recv()
            rows = pl.ds(*SUM_ROWS[i][t])
            total = sums[ph, rows, :] + got[ph, 0, rows, :] + got[ph, 1, rows, :] + got[ph, 2, rows, :]
            if ph < 2:
                sums[ph + 1, rows, :] = total
            else:
                scale[rows, :] = mag[rows, :] / jnp.sqrt(total + EPS)

    stages = ((sg, s1g, s2g, og), (su, s1u, s2u, ou), (sd, s1d, s2d, od))

    def far_copy(g, ph, t, k):
        m, thirds = GROUPS[g]
        axis = ORDERS[t][ph]
        p, mine, other = peer_of(me, axis, k)
        return pltpu.make_async_remote_copy(
            src_ref=at(stages[m][ph], axis, other, thirds[t]),
            dst_ref=at(stages[m][ph + 1], axis, mine, thirds[t]),
            send_sem=x_send.at[g, ph, t, k - 1], recv_sem=x_recv.at[g, ph, t, k - 1],
            device_id=(p, core), device_id_type=MESH,
        )

    def near_copy(g, ph, t):
        m, thirds = GROUPS[g]
        axis = ORDERS[t][ph]
        _, mine, _ = peer_of(me, axis, 1)
        return pltpu.make_async_copy(
            at(stages[m][ph], axis, mine, thirds[t]),
            at(stages[m][ph + 1], axis, mine, thirds[t]),
            x_loc.at[g, ph, t],
        )

    def arrive(g, ph, t):
        for k in (2, 1, 3):
            far_copy(g, ph, t, k).wait_recv()
        near_copy(g, ph, t).wait()

    def send(g, ph):
        for t in range(3):
            if ph > 0:
                arrive(g, ph - 1, t)
            for k in (2, 1, 3):
                far_copy(g, ph, t, k).start()
            near_copy(g, ph, t).start()

    weights = ((vg, rg, both_g, sg), (vu, ru, both_u, su))
    blocks = COLS // BLK
    tail = blocks * BLK

    def square_blocks(i, lo, hi, last, keep):
        w, q, both, _ = weights[i]
        p = both[...].reshape(2 * RANK, RANK)

        def body(b, carry):
            start = pl.multiple_of(b * BLK, BLK)
            x = combined_t(w, q, p, start, BLK)
            if keep:
                full[pl.ds(start, BLK), :] = x
            sums[0, pl.ds(pl.multiple_of(FIRST[i] + b * 8, 8), 8), :] = to_lanes(x * x)
            return carry

        lax.fori_loop(lo, hi, body, 0)
        if last:
            x = combined_t(w, q, p, tail, COLS - tail)
            if keep:
                full[tail:COLS, :] = x
            sums[0, FIRST[i] + 112 : FIRST[i] + 116, :] = to_lanes(x * x)
            sums[0, FIRST[i] + 116 : FIRST[i] + 120, :] = jnp.zeros((4, 128), F32)

    def scale_blocks(i, kept):
        w, q, both, _ = weights[i]
        p = both[...].reshape(2 * RANK, RANK)

        def body(b, carry):
            start = pl.multiple_of(b * BLK, BLK)
            x = full[pl.ds(start, BLK), :] if kept else combined_t(w, q, p, start, BLK)
            f = scale[pl.ds(pl.multiple_of(FIRST[i] + b * 8, 8), 8), :]
            for e in range(8):
                full[pl.ds(pl.multiple_of(start + e * 128, 128), 128), :] = x[
                    e * 128 : (e + 1) * 128
                ] * to_sublanes(f[e : e + 1], 128)
            return carry

        lax.fori_loop(0, blocks, body, 0)
        x = full[tail:COLS, :] if kept else combined_t(w, q, p, tail, COLS - tail)
        f = scale[FIRST[i] + 112 : FIRST[i] + 116, :]
        for e in range(4):
            h = 128 if e < 3 else 64
            full[tail + e * 128 : tail + e * 128 + h, :] = x[
                e * 128 : e * 128 + h
            ] * to_sublanes(f[e : e + 1], h)

    def cut(i):
        s = weights[i][3]

        def body(g, carry):
            base = pl.multiple_of(g * (8 * SLAB), 8)
            for e in range(8):
                s[lax.div(g, 2), lax.rem(g, 2) * 2 + e // 4, e % 4] = full[
                    pl.ds(base + e * SLAB, SLAB + 1), :
                ].astype(BF)
            return carry

        lax.fori_loop(0, N // 8, body, 0)

    def down_block(j):
        lanes = pl.ds(pl.multiple_of(j * 128, 128), 128)
        p = pdown[0:DROWS, :].astype(BF)
        upd = jnp.dot(p, rd[:, lanes], preferred_element_type=F32)
        return vd[:, lanes].astype(F32) + upd

    def square_down(j, carry):
        x = down_block(j)
        sums[0, pl.ds(FIRST[2] + j, 1), :] = jnp.sum(x * x, axis=0, keepdims=True)
        return carry

    first = WINDOW - lax.rem(me * DROWS, WINDOW)

    def merge_down(j, carry):
        y = down_block(j) * scale[pl.ds(FIRST[2] + j, 1), :]
        turn[0:DROWS, :] = y
        turn[WINDOW : WINDOW + DROWS, :] = y
        z = turn[pl.ds(first, WINDOW), :].T.astype(BF)
        a, b, c = lax.div(j, 8), lax.rem(lax.div(j, 2), 4), lax.rem(j, 2) * 2
        for e in range(4):
            sd[a, b, c, e * 64 : (e + 1) * 64, :] = z[0:64, e * 128 : (e + 1) * 128]
            sd[a, b, c + 1, e * 64 : (e + 1) * 64, :] = z[64:128, e * 128 : (e + 1) * 128]
        return carry

    full[COLS : COLS + 8, :] = jnp.zeros((8, 128), F32)
    turn[...] = jnp.zeros_like(turn)
    q_load[0].wait()
    w_load[0][0].wait()
    square_blocks(0, 0, 7, False, True)
    w_load[0][1].wait()
    square_blocks(0, 7, blocks, True, True)
    send_sums(0, 0)
    q_load[1].wait()
    w_load[1][0].wait()
    square_blocks(1, 0, 7, False, False)
    take_sums(0, 0)
    send_sums(0, 1)
    w_load[1][1].wait()
    square_blocks(1, 7, blocks, True, False)
    take_sums(0, 1)
    send_sums(0, 2)
    send_sums(1, 0)
    pdown[0:231, :] = both_d[0].astype(F32).T
    pdown[231:462, :] = both_d[1].astype(F32).T
    q_load[2].wait()
    w_load[2][0].wait()
    lax.fori_loop(0, 12, square_down, 0)
    mag_load.wait()
    take_sums(0, 2)
    take_sums(1, 0)
    send_sums(1, 1)
    scale_blocks(0, True)
    take_sums(1, 1)
    send_sums(1, 2)
    cut(0)
    send(0, 0)
    lax.fori_loop(12, DCOLS // 128, square_down, 0)
    send_sums(2, 0)
    take_sums(1, 2)
    scale_blocks(1, False)
    cut(1)
    send(1, 0)
    take_sums(2, 0)
    send_sums(2, 1)
    send(0, 1)
    take_sums(2, 1)
    send_sums(2, 2)
    send(1, 1)
    send(0, 2)
    take_sums(2, 2)
    lax.fori_loop(0, DCOLS // 128, merge_down, 0)
    send(2, 0)
    send(3, 0)
    send(1, 2)
    for ph in (1, 2):
        send(2, ph)
        send(3, ph)
    for g in range(4):
        for t in range(3):
            arrive(g, 2, t)
    for g in range(4):
        for ph in range(3):
            for t in range(3):
                for k in (1, 2, 3):
                    far_copy(g, ph, t, k).wait_send()
    for i in range(3):
        for ph in range(3):
            for t in range(3):
                for k in (1, 2, 3):
                    sum_copy(i, ph, t, k).wait_send()


def merge(wg, wu, wd, qg, qu, qd, pg, pu, pd, mags):
    hbm = pl.BlockSpec(memory_space=pl.ANY)
    vmem = pl.BlockSpec(memory_space=pltpu.VMEM)
    slab = (4, 4, 4, SLAB + 1, 128)
    dslab = (4, 4, 4, 256, 128)
    shapes = (slab, slab, dslab)
    dma = pltpu.SemaphoreType.DMA
    return pl.pallas_call(
        merge_kernel,
        out_shape=[pltpu.VMEM(s, BF) for s in shapes]
        + [jax.ShapeDtypeStruct(s, BF) for s in shapes],
        in_specs=[hbm] * 6 + [vmem] * 3 + [hbm],
        out_specs=[vmem] * 3 + [hbm] * 3,
        scratch_shapes=[
            pltpu.VMEM((COLS, 128), BF), pltpu.VMEM((COLS, 128), BF),
            pltpu.VMEM((DROWS, DCOLS), BF),
            pltpu.VMEM((RANK, COLS), BF), pltpu.VMEM((RANK, COLS), BF),
            pltpu.VMEM((RANK, DCOLS), BF),
            *[pltpu.VMEM(s, BF) for s in shapes * 2],
            pltpu.VMEM((COLS + 8, 128), F32), pltpu.VMEM((2 * WINDOW, 128), F32),
            pltpu.VMEM((2, 64, 64), BF), pltpu.VMEM((2, 64, 64), BF), pltpu.VMEM((2, 64, 231), BF),
            pltpu.VMEM((464, 64), F32), pltpu.VMEM((272, 128), F32),
            pltpu.VMEM((3, 272, 128), F32), pltpu.VMEM((3, 3, 272, 128), F32),
            pltpu.VMEM((272, 128), F32),
            dma((3, 2)), dma((4,)), dma((3,)), dma((3,)), dma((3,)),
            dma((3, 3, 3, 3)), dma((3, 3, 3, 3)),
            dma((4, 3, 3, 3)), dma((4, 3, 3, 3)), dma((4, 3, 3)),
        ],
        compiler_params=pltpu.CompilerParams(
            collective_id=0, has_side_effects=True, vmem_limit_bytes=52 * 10**6
        ),
        name="merge",
    )(wg, wu, wd, qg, qu, qd, pg, pu, pd, mags)[:3]


def join_kernel(x, o):
    first = pl.program_id(0) * 8
    for e in range(8):
        o[:, e * 128 : (e + 1) * 128] = x[first + e, 0:SLAB, :]


def join(x):
    return pl.pallas_call(
        join_kernel,
        grid=(N // 8,),
        out_shape=jax.ShapeDtypeStruct((SLAB, N * 128), BF),
        in_specs=[pl.BlockSpec(memory_space=pltpu.VMEM)],
        out_specs=pl.BlockSpec((SLAB, 1024), lambda i: (0, i)),
        compiler_params=pltpu.CompilerParams(vmem_limit_bytes=16 * 2**20),
        name="join",
    )(x.reshape(N, SLAB + 1, 128))


TILES = 33


def join_down_kernel(x, o):
    g = pl.program_id(0)

    def tile(i, carry):
        t = g * TILES + i
        s = lax.div(t * 128, DROWS)
        nxt = jnp.minimum(s + 1, N - 1)
        rows = pl.ds(pl.multiple_of(lax.rem(t, 4) * 64, 64), 64)
        lane = t * 128 + lax.broadcasted_iota(jnp.int32, (64, 128), 1)
        a = x[s, rows, :]
        b = x[nxt, rows, :]
        o[:, pl.ds(pl.multiple_of(i * 128, 128), 128)] = jnp.where(lane < (s + 1) * DROWS, a, b)
        return carry

    lax.fori_loop(0, TILES, tile, 0)


def join_down(x):
    return pl.pallas_call(
        join_down_kernel,
        grid=(7,),
        out_shape=jax.ShapeDtypeStruct((64, 29568), BF),
        in_specs=[pl.BlockSpec(memory_space=pltpu.VMEM)],
        out_specs=pl.BlockSpec((64, TILES * 128), lambda i: (0, i)),
        compiler_params=pltpu.CompilerParams(vmem_limit_bytes=16 * 2**20),
        name="join_down",
    )(x.reshape(N, 256, 128))


def local(wg, wu, wd, pg, qg, pu, qu, pd, qd, mg, mu, md):
    pad = jnp.zeros((15360 - COLS,), F32)
    mags = jnp.concatenate((mg, pad, mu, pad, md)).reshape(272, 128)
    g, u, d = merge(wg.T, wu.T, wd, qg, qu, qd, pg, pu, pd.T, mags)
    return join(g).T, join(u).T, join_down(d).T


def solution(mesh):
    placed = (
        P("row", "col"),
        P("row", "col"),
        P("row", "col"),
        P(("row", "col"), None),
        P(None, "col"),
        P(("row", "col"), None),
        P(None, "col"),
        P(("row", "col"), None),
        P(None, "col"),
        P("col"),
        P("col"),
        P("col"),
    )
    return jax.shard_map(
        local,
        mesh=mesh,
        in_specs=placed,
        out_specs=(P(None, ("col", "row")), P(None, ("col", "row")), P(None, ("col", "row"))),
        check_vma=False,
    )
```

time: 317 us -> 180 us (0.57); the launches traced: 312 us -> 180 us
  Pallas kernels: 0 us -> 177 us
  waiting for transfers between devices: 158 us -> 0 us
  local copies, waits for them, and re-layouts: 74.5 us -> 1.59 us
  starting transfers between devices: 31.5 us -> 0 us
  other arithmetic: 18.4 us -> 0 us
  matrix products: 16 us -> 0 us
  between operations: 14.3 us -> 0.65 us
    pallas_call x0 -> x4, Pallas kernels: none -> 177 us  [the longest x1 164 us: merge(): pl.pallas_call(merge_kernel, out_shape=[pltpu.VMEM(s, BF) for s in shapes...]
    all_to_all x3 -> x0, waiting for transfers between devices: 104 us -> none  [the longest x1 42.9 us: local(): lax.all_to_all(up_weight, 'row', split_axis=1, concat_axis=0, tiled=True)]
    all_gather x2 -> x0, waiting for transfers between devices: 53.1 us -> none  [the longest x1 50.8 us: local(): lax.all_gather(down_in, ('row', 'col'), axis=0, tiled=True)]
    unnamed x14 -> x0, local copies, waits for them, and re-layouts: 37.3 us -> none
    all_to_all x3 -> x0, starting transfers between devices: 31.3 us -> none  [the longest x1 12.2 us: local(): lax.all_to_all(up_weight, 'row', split_axis=1, concat_axis=0, tiled=True)]
    convert_element_type x4 -> x0, local copies, waits for them, and re-layouts: 20.7 us -> none  [combine_update(): return weight.astype(jnp.float32) + update]
    convert_element_type x6 -> x0, other arithmetic: 16.2 us -> none  [the longest x3 8.58 us: combine_update(): return weight.astype(jnp.float32) + update]
    dot_general x3 -> x0, matrix products: 16 us -> none  [combine_update(): jnp.dot(factor_rows, factor_cols, preferred_element_type=jnp.float32)]
  transfers between devices with their start and end apart: 5 -> 0, of which waited for: 5 -> 0; matrix products, arithmetic and copies ran while one was open for 24% -> 0% of each run, Pallas kernels for 0% -> 0%
where the time goes in v2:
time: 180 us
  Pallas kernels  177 us (98%)
    pallas_call x1, Pallas kernels, merge(): pl.pallas_call(merge_kernel, out_shape=[pltpu.VMEM(s, BF) for s in shapes...  164 us
    pallas_call x2, Pallas kernels, join(): pl.pallas_call(join_kernel, grid=(N // 8,), out_shape=jax.ShapeDtypeStruc...  7.57 us
    pallas_call x1, Pallas kernels, join_down(): pl.pallas_call(join_down_kernel, grid=(7,), out_shape=jax.ShapeDtypeStruc...  5.35 us

profile of v2, /device:TPU:1, one launch (start us, length us, event | category | flops | bytes accessed | tf_op | source)
XLA Modules:
  0.0 179.6 jit_solution(9845456320710051474)
XLA Ops:
  0.6 1.6 concatenate.3
  2.2 164.5 %merge.1 = (bf16[4,4,4,232,128]{4,3,2,1,0:T(8,128)(2,1)S(1)}, bf16[4,4,4,232,128]{4,3,2,1,0:T(8,128)(2,1)S(1)}, bf16[4,4,4,256,128]{4,3,2,1,0:T(8,128)(2,1)S(1)}...) custom-call(bf16[14784,128]{1,0:T(8,128)(2,1)} %bitcast.15, ...), custom_call_target="tpu_custom_call" | custom-call | tf_op jit(solution)/shard_map/merge/pallas_call | solution.py:353
  166.7 3.8 %join.2 = bf16[231,8192]{1,0:T(8,128)(2,1)} custom-call(bf16[64,232,128]{2,1,0:T(8,128)(2,1)S(1)} %bitcast.12), custom_call_target="tpu_custom_call" | custom-call | tf_op jit(solution)/shard_map/join/pallas_call | solution.py:388
  170.5 3.8 %join.3 = bf16[231,8192]{1,0:T(8,128)(2,1)} custom-call(bf16[64,232,128]{2,1,0:T(8,128)(2,1)S(1)} %bitcast.11), custom_call_target="tpu_custom_call" | custom-call | tf_op jit(solution)/shard_map/join/pallas_call | solution.py:388
  174.3 5.4 %join_down.1 = bf16[64,29568]{1,0:T(8,128)(2,1)} custom-call(bf16[64,256,128]{2,1,0:T(8,128)(2,1)S(1)} %bitcast.10), custom_call_target="tpu_custom_call" | custom-call | tf_op jit(solution)/shard_map/join_down/pallas_call | solution.py:420
  (1 shorter events, 0.0 us)

commit v3 on v2

v3 whole, which is shorter than its diff:
```python
import functools

import jax
import jax.numpy as jnp
from jax import lax
from jax.experimental import pallas as pl
from jax.experimental.pallas import tpu as pltpu
from jax.sharding import PartitionSpec as P

MESH = pl.DeviceIdType.MESH
BF = jnp.bfloat16
F32 = jnp.float32
EPS = 1e-06
RANK = 64
N = 64
COLS = 14784
SLAB = 231
DROWS = 462
DCOLS = 4096
WINDOW = 512
WIDE = 240
BLK = 1024
HALF = 8 * BLK
ORDERS = ((2, 1, 0), (1, 0, 2), (0, 2, 1))
FIRST = (0, 120, 240)
SUM_ROWS = (
    None,
    ((120, 40), (160, 40), (200, 40)),
    ((240, 8), (248, 8), (256, 16)),
)
GROUPS = (
    (0, ((0, 48), (80, 48), (160, 48))),
    (0, ((48, 32), (128, 32), (208, 32))),
    (1, ((0, 48), (80, 48), (160, 48))),
    (1, ((48, 32), (128, 32), (208, 24))),
    (2, ((0, 48), (80, 48), (176, 48))),
    (2, ((48, 32), (128, 48), (224, 32))),
)
P_ROWS = ((0, 32), (32, 16), (48, 16))


def peer_of(me, axis, k):
    stride = (16, 4, 1)[axis]
    mine = lax.rem(lax.div(me, stride), 4)
    other = lax.rem(mine + k, 4)
    return me + (other - mine) * stride, mine, other


def greet(me, core):
    bar = pltpu.get_barrier_semaphore()
    for axis in range(3):
        for k in (1, 2, 3):
            p, _, _ = peer_of(me, axis, k)
            pl.semaphore_signal(bar, inc=1, device_id=(p, core), device_id_type=MESH)
    pl.semaphore_signal(bar, inc=1, device_id=(me, 1 - core), device_id_type=MESH)
    pl.semaphore_wait(bar, 10)


def eye(h):
    return lax.broadcasted_iota(jnp.int32, (h, 128), 0) == lax.broadcasted_iota(
        jnp.int32, (h, 128), 1
    )


def to_lanes(x):
    n = x.shape[0]
    sums = jnp.sum(x, axis=1, keepdims=True)
    rows = []
    for b in range(0, n, 128):
        h = min(128, n - b)
        rows.append(jnp.sum(jnp.where(eye(h), sums[b : b + h], 0.0), axis=0, keepdims=True))
    return jnp.concatenate(rows, axis=0)


def to_sublanes(row, h):
    return jnp.sum(jnp.where(eye(h), row, 0.0), axis=1, keepdims=True)


def combined_t(w, q, p, start, n):
    upd = lax.dot_general(
        q[:, pl.ds(start, n)], p, (((0,), (1,)), ((), ())), preferred_element_type=F32
    )
    return w[pl.ds(start, n), :].astype(F32) + upd


def at(ref, axis, idx, rows):
    ix = [slice(None)] * 3
    ix[axis] = idx
    return ref.at[(*ix, pl.ds(*rows))]


def window(s):
    return jnp.minimum(lax.div(s * SLAB, 8) * 8, COLS - WIDE)


def merge_kernel(
    wg, wu, wd, qg, qu, qd, pg, pu, pd, mags,
    og, ou, od, s1u, s1d,
    vu, vd, rg, ru, rd, su, sd, s1g, s2g, s3g, s2u, s2d,
    full, turn, both_g, both_u, both_d, pdown, mag, sums, got, scale,
    gathered, qwin, qcol, mcol, acc, shift,
    w_sem, q_sem, p_send, p_recv, p_loc, r_send, r_recv, x_send, x_recv, x_loc,
    g_send, g_recv,
):
    me = lax.axis_index("row")
    core = lax.axis_index("col")
    mine_at = (lax.div(me, 16), lax.rem(lax.div(me, 4), 4), lax.rem(me, 4))
    half = 7 * BLK
    u_loads = [
        pltpu.make_async_copy(wu.at[part], vu.at[part], w_sem.at[h])
        for h, part in enumerate((pl.ds(0, half), pl.ds(half, COLS - half)))
    ]
    d_load = pltpu.make_async_copy(wd, vd, w_sem.at[2])
    q_loads = [
        pltpu.make_async_copy(src, dst, q_sem.at[i])
        for i, (src, dst) in enumerate(((qg, rg), (qu, ru), (qd, rd), (mags, mag)))
    ]
    q_loads[1].start()
    u_loads[0].start()
    greet(me, core)
    ps = []
    for i, (src, dst) in enumerate(((pg, both_g), (pu, both_u), (pd, both_d))):
        far = pltpu.make_async_remote_copy(
            src_ref=src, dst_ref=dst.at[core], send_sem=p_send.at[i], recv_sem=p_recv.at[i],
            device_id=(me, 1 - core), device_id_type=MESH,
        )
        near = pltpu.make_async_copy(src, dst.at[core], p_loc.at[i])
        far.start()
        near.start()
        ps.append((far, near))

    def sum_copy(i, ph, t, k):
        q, _, _ = peer_of(me, ORDERS[t][ph], k)
        rows = pl.ds(*SUM_ROWS[i][t])
        return pltpu.make_async_remote_copy(
            src_ref=sums.at[ph, rows], dst_ref=got.at[ph, k - 1, rows],
            send_sem=r_send.at[i, ph, t, k - 1], recv_sem=r_recv.at[i, ph, t, k - 1],
            device_id=(q, core), device_id_type=MESH,
        )

    def send_sums(i, ph):
        for t in range(3):
            for k in (2, 1, 3):
                sum_copy(i, ph, t, k).start()

    def take_sums(i, ph):
        for t in range(3):
            for k in (2, 1, 3):
                sum_copy(i, ph, t, k).wait_recv()
            rows = pl.ds(*SUM_ROWS[i][t])
            total = sums[ph, rows, :] + got[ph, 0, rows, :] + got[ph, 1, rows, :] + got[ph, 2, rows, :]
            if ph < 2:
                sums[ph + 1, rows, :] = total
            else:
                scale[rows, :] = mag[rows, :] / jnp.sqrt(total + EPS)

    stages = ((s1g, s1g, s2g, s3g), (su, s1u, s2u, ou), (sd, s1d, s2d, od))

    def far_copy(g, ph, t, k):
        m, thirds = GROUPS[g]
        axis = ORDERS[t][ph]
        p, mine, other = peer_of(me, axis, k)
        return pltpu.make_async_remote_copy(
            src_ref=at(stages[m][ph], axis, other, thirds[t]),
            dst_ref=at(stages[m][ph + 1], axis, mine, thirds[t]),
            send_sem=x_send.at[g, ph, t, k - 1], recv_sem=x_recv.at[g, ph, t, k - 1],
            device_id=(p, core), device_id_type=MESH,
        )

    def near_copy(g, ph, t):
        m, thirds = GROUPS[g]
        axis = ORDERS[t][ph]
        _, mine, _ = peer_of(me, axis, 1)
        return pltpu.make_async_copy(
            at(stages[m][ph], axis, mine, thirds[t]),
            at(stages[m][ph + 1], axis, mine, thirds[t]),
            x_loc.at[g, ph, t],
        )

    def arrive(g, ph, t):
        for k in (2, 1, 3):
            far_copy(g, ph, t, k).wait_recv()
        near_copy(g, ph, t).wait()

    def send(g, ph):
        for t in range(3):
            if ph > 0:
                arrive(g, ph - 1, t)
            for k in (2, 1, 3):
                far_copy(g, ph, t, k).start()
            near_copy(g, ph, t).start()

    def send_gate(g):
        for t, rows in enumerate(GROUPS[g][1]):
            axis = ORDERS[t][0]

            def place(i, value, axis=axis):
                ix = [lax.div(i, 4), lax.rem(i, 4)]
                ix.insert(axis, value)
                return ix

            def src(i, value, rows=rows, place=place):
                z, y, x = place(i, value)
                start = window(z * 16 + y * 4 + x) + rows[0]
                return wg.at[pl.ds(pl.multiple_of(start, 8), rows[1])]

            def go(i, carry, axis=axis, rows=rows, place=place, src=src, t=t):
                for k in (2, 1, 3):
                    p, mine, other = peer_of(me, axis, k)
                    pltpu.make_async_remote_copy(
                        src_ref=src(i, other),
                        dst_ref=s1g.at[(*place(i, mine), pl.ds(*rows))],
                        send_sem=x_send.at[g, 0, t, k - 1], recv_sem=x_recv.at[g, 0, t, k - 1],
                        device_id=(p, core), device_id_type=MESH,
                    ).start()
                _, mine, _ = peer_of(me, axis, 1)
                pltpu.make_async_copy(
                    src(i, mine), s1g.at[(*place(i, mine), pl.ds(*rows))], x_loc.at[g, 0, t]
                ).start()
                return carry

            lax.fori_loop(0, 16, go, 0)

    def factor_copy(ph, t, k):
        axis = ORDERS[t][ph]
        p, _, _ = peer_of(me, axis, k)
        ix = list(mine_at)
        for done in ORDERS[t][:ph]:
            ix[done] = slice(None)
        block = gathered.at[(*ix, pl.ds(*P_ROWS[t]))]
        return pltpu.make_async_remote_copy(
            src_ref=block, dst_ref=block,
            send_sem=g_send.at[ph, t, k - 1], recv_sem=g_recv.at[ph, t, k - 1],
            device_id=(p, core), device_id_type=MESH,
        )

    def send_factor(ph):
        for t in range(3):
            for k in (2, 1, 3):
                factor_copy(ph, t, k).start()

    def take_factor(ph):
        for t in range(3):
            for k in (2, 1, 3):
                factor_copy(ph, t, k).wait_recv()

    def source(i):
        return lax.div(i, 16), lax.rem(lax.div(i, 4), 4), lax.rem(i, 4)

    start = window(me)
    tile = lax.div(start, 128)
    inner = pl.multiple_of(start - tile * 128, 8)
    skip = me * SLAB - start

    def own_columns():
        @pl.when(me < N - 1)
        def _():
            qwin[...] = rg[:, pl.ds(pl.multiple_of(tile * 128, 128), 384)].astype(F32).T

        @pl.when(me == N - 1)
        def _():
            qwin[0:320, :] = rg[:, COLS - 320 : COLS].astype(F32).T

        qcol[...] = qwin[pl.ds(inner, WIDE), :].astype(BF)
        for e in range(3):
            mcol[e * 128 : (e + 1) * 128, :] = jnp.broadcast_to(
                to_sublanes(mag[pl.ds(tile + e, 1), :], 128), (128, 128)
            )

    def gate_block(i):
        z, y, x = source(i)
        upd = jnp.dot(qcol[...], gathered[z, y, x], preferred_element_type=F32)
        return s3g[z, y, x].astype(F32) + upd

    def gate_squares(i, carry):
        x = gate_block(i)
        acc[...] += x * x
        return carry

    def gate_scale():
        total = jnp.sum(acc[...], axis=1, keepdims=True)
        acc[...] = mcol[pl.ds(inner, WIDE), :] / jnp.sqrt(total + EPS)

    def gate_finish(i, carry):
        shift[0:WIDE, :] = gate_block(i) * acc[...]
        og[:, pl.ds(pl.multiple_of(i * 128, 128), 128)] = shift[pl.ds(skip, SLAB), :].astype(BF)
        return carry

    blocks = COLS // BLK
    tail = blocks * BLK

    def square_blocks(lo, hi, last):
        p = both_u[...].reshape(2 * RANK, RANK)

        def body(b, carry):
            x = combined_t(vu, ru, p, pl.multiple_of(b * BLK, BLK), BLK)
            sums[0, pl.ds(pl.multiple_of(FIRST[1] + b * 8, 8), 8), :] = to_lanes(x * x)
            return carry

        lax.fori_loop(lo, hi, body, 0)
        if last:
            x = combined_t(vu, ru, p, tail, COLS - tail)
            sums[0, FIRST[1] + 112 : FIRST[1] + 116, :] = to_lanes(x * x)
            sums[0, FIRST[1] + 116 : FIRST[1] + 120, :] = jnp.zeros((4, 128), F32)

    def merge_up(h):
        p = both_u[...].reshape(2 * RANK, RANK)
        lo = 7 * h

        def body(b, carry):
            start = pl.multiple_of(b * BLK, BLK)
            x = combined_t(vu, ru, p, start, BLK)
            f = scale[pl.ds(pl.multiple_of(FIRST[1] + b * 8, 8), 8), :]
            for e in range(8):
                to = pl.multiple_of(start - lo * BLK + e * 128, 128)
                full[pl.ds(to, 128), :] = x[e * 128 : (e + 1) * 128] * to_sublanes(f[e : e + 1], 128)
            return carry

        lax.fori_loop(lo, 8 if h == 0 else blocks, body, 0)
        if h == 1:
            x = combined_t(vu, ru, p, tail, COLS - tail)
            f = scale[FIRST[1] + 112 : FIRST[1] + 116, :]
            for e in range(4):
                n = 128 if e < 3 else 64
                to = tail - lo * BLK + e * 128
                full[to : to + n, :] = x[e * 128 : e * 128 + n] * to_sublanes(f[e : e + 1], n)
            end = COLS - lo * BLK
            full[end : end + 8, :] = jnp.zeros((8, 128), F32)

        def cut(g, carry):
            base = pl.multiple_of(g * (8 * SLAB) - lo * BLK, 8)
            for e in range(8):
                su[lax.div(g, 2), lax.rem(g, 2) * 2 + e // 4, e % 4] = full[
                    pl.ds(base + e * SLAB, SLAB + 1), :
                ].astype(BF)
            return carry

        lax.fori_loop(4 * h, 4 * h + 4, cut, 0)

    def down_block(j):
        lanes = pl.ds(pl.multiple_of(j * 128, 128), 128)
        p = pdown[0:DROWS, :].astype(BF)
        upd = jnp.dot(p, rd[:, lanes], preferred_element_type=F32)
        return vd[:, lanes].astype(F32) + upd

    def square_down(j, carry):
        x = down_block(j)
        sums[0, pl.ds(FIRST[2] + j, 1), :] = jnp.sum(x * x, axis=0, keepdims=True)
        return carry

    first = WINDOW - lax.rem(me * DROWS, WINDOW)

    def merge_down(j, carry):
        y = down_block(j) * scale[pl.ds(FIRST[2] + j, 1), :]
        turn[0:DROWS, :] = y
        turn[WINDOW : WINDOW + DROWS, :] = y
        z = turn[pl.ds(first, WINDOW), :].T.astype(BF)
        a, b, c = lax.div(j, 8), lax.rem(lax.div(j, 2), 4), lax.rem(j, 2) * 2
        for e in range(4):
            sd[a, b, c, e * 64 : (e + 1) * 64, :] = z[0:64, e * 128 : (e + 1) * 128]
            sd[a, b, c + 1, e * 64 : (e + 1) * 64, :] = z[64:128, e * 128 : (e + 1) * 128]
        return carry

    send_gate(0)
    send_gate(1)
    u_loads[1].start()
    q_loads[2].start()
    d_load.start()
    q_loads[3].start()
    q_loads[0].start()
    for far, near in ps:
        near.wait()
        far.wait()
    turn[...] = jnp.zeros_like(turn)
    acc[...] = jnp.zeros_like(acc)
    qwin[...] = jnp.zeros_like(qwin)
    gathered[mine_at] = both_g[...].reshape(2 * RANK, RANK).astype(F32).T.astype(BF)
    q_loads[1].wait()
    u_loads[0].wait()
    square_blocks(0, 7, False)
    send_factor(0)
    u_loads[1].wait()
    square_blocks(7, blocks, True)
    pdown[0:231, :] = both_d[0].astype(F32).T
    pdown[231:462, :] = both_d[1].astype(F32).T
    send_sums(1, 0)
    send(0, 1)
    q_loads[2].wait()
    d_load.wait()
    lax.fori_loop(0, 12, square_down, 0)
    take_factor(0)
    send_factor(1)
    q_loads[3].wait()
    take_sums(1, 0)
    send_sums(1, 1)
    send(1, 1)
    lax.fori_loop(12, DCOLS // 128, square_down, 0)
    send_sums(2, 0)
    take_sums(1, 1)
    send_sums(1, 2)
    send(0, 2)
    take_factor(1)
    send_factor(2)
    take_sums(1, 2)
    send(1, 2)
    merge_up(0)
    merge_up(1)
    take_sums(2, 0)
    send_sums(2, 1)
    send(2, 0)
    send(3, 0)
    q_loads[0].wait()
    own_columns()
    take_factor(2)
    for t in range(3):
        arrive(0, 2, t)
        arrive(1, 2, t)
    lax.fori_loop(0, N, gate_squares, 0)
    gate_scale()
    take_sums(2, 1)
    send_sums(2, 2)
    send(2, 1)
    lax.fori_loop(0, N, gate_finish, 0)
    send(3, 1)
    take_sums(2, 2)
    lax.fori_loop(0, DCOLS // 256, merge_down, 0)
    send(2, 2)
    lax.fori_loop(DCOLS // 256, DCOLS // 128, merge_down, 0)
    send(4, 0)
    send(5, 0)
    send(3, 2)
    for ph in (1, 2):
        send(4, ph)
        send(5, ph)
    for g in range(2, 6):
        for t in range(3):
            arrive(g, 2, t)
    for g in range(6):
        for ph in range(3):
            for t in range(3):
                for k in (1, 2, 3):
                    far_copy(g, ph, t, k).wait_send()
    for ph in range(3):
        for t in range(3):
            for k in (1, 2, 3):
                sum_copy(1, ph, t, k).wait_send()
                sum_copy(2, ph, t, k).wait_send()
                factor_copy(ph, t, k).wait_send()


def merge(wg, wu, wd, qg, qu, qd, pg, pu, pd, mags):
    hbm = pl.BlockSpec(memory_space=pl.ANY)
    vmem = pl.BlockSpec(memory_space=pltpu.VMEM)
    wide = (4, 4, 4, WIDE, 128)
    slab = (4, 4, 4, SLAB + 1, 128)
    dslab = (4, 4, 4, 256, 128)
    dma = pltpu.SemaphoreType.DMA
    return pl.pallas_call(
        merge_kernel,
        out_shape=[pltpu.VMEM(s, BF) for s in ((SLAB, N * 128), slab, dslab)]
        + [jax.ShapeDtypeStruct(s, BF) for s in (slab, dslab)],
        in_specs=[hbm] * 6 + [vmem] * 3 + [hbm],
        out_specs=[vmem] * 3 + [hbm] * 2,
        scratch_shapes=[
            pltpu.VMEM((COLS, 128), BF), pltpu.VMEM((DROWS, DCOLS), BF),
            pltpu.VMEM((RANK, COLS), BF), pltpu.VMEM((RANK, COLS), BF),
            pltpu.VMEM((RANK, DCOLS), BF),
            *[pltpu.VMEM(s, BF) for s in (slab, dslab, wide, wide, wide, slab, dslab)],
            pltpu.VMEM((HALF, 128), F32), pltpu.VMEM((2 * WINDOW, 128), F32),
            pltpu.VMEM((2, 64, 64), BF), pltpu.VMEM((2, 64, 64), BF), pltpu.VMEM((2, 64, 231), BF),
            pltpu.VMEM((464, 64), F32), pltpu.VMEM((272, 128), F32),
            pltpu.VMEM((3, 272, 128), F32), pltpu.VMEM((3, 3, 272, 128), F32),
            pltpu.VMEM((272, 128), F32),
            pltpu.VMEM((4, 4, 4, RANK, 128), BF), pltpu.VMEM((384, RANK), F32),
            pltpu.VMEM((WIDE, RANK), BF), pltpu.VMEM((384, 128), F32),
            pltpu.VMEM((WIDE, 128), F32), pltpu.VMEM((WIDE + 8, 128), F32),
            dma((3,)), dma((4,)), dma((3,)), dma((3,)), dma((3,)),
            dma((3, 3, 3, 3)), dma((3, 3, 3, 3)),
            dma((6, 3, 3, 3)), dma((6, 3, 3, 3)), dma((6, 3, 3)),
            dma((3, 3, 3)), dma((3, 3, 3)),
        ],
        compiler_params=pltpu.CompilerParams(
            collective_id=0, has_side_effects=True, vmem_limit_bytes=54 * 10**6
        ),
        name="merge",
    )(wg, wu, wd, qg, qu, qd, pg, pu, pd, mags)[:3]


LANES = 1024
TILES = 33
DEPTH = 4


def join_kernel(g, u, d, og, ou, od, bufs, dbufs, gsem, sem, dsem):
    gate = pltpu.make_async_copy(g, og, gsem)
    gate.start()

    def out_down(i):
        lanes = pl.ds(pl.multiple_of(i * (TILES * 128), 128), TILES * 128)
        b = lax.rem(i, DEPTH)
        return pltpu.make_async_copy(dbufs.at[b], od.at[:, lanes], dsem.at[b])

    def step_down(i, carry):
        @pl.when(i >= DEPTH)
        def _():
            out_down(i - DEPTH).wait()

        buf = dbufs.at[lax.rem(i, DEPTH)]

        def tile(j, carry):
            t = i * TILES + j
            s = lax.div(t * 128, DROWS)
            nxt = jnp.minimum(s + 1, N - 1)
            rows = pl.ds(pl.multiple_of(lax.rem(t, 4) * 64, 64), 64)
            lane = t * 128 + lax.broadcasted_iota(jnp.int32, (64, 128), 1)
            buf[:, pl.ds(pl.multiple_of(j * 128, 128), 128)] = jnp.where(
                lane < (s + 1) * DROWS, d[s, rows, :], d[nxt, rows, :]
            )
            return carry

        lax.fori_loop(0, TILES, tile, 0, unroll=11)
        out_down(i).start()
        return carry

    lax.fori_loop(0, 7, step_down, 0)

    def out(i):
        b = lax.rem(i, DEPTH)
        lanes = pl.ds(pl.multiple_of(i * LANES, LANES), LANES)
        return pltpu.make_async_copy(bufs.at[b], ou.at[:, lanes], sem.at[b])

    def step(i, carry):
        @pl.when(i >= DEPTH)
        def _():
            out(i - DEPTH).wait()

        buf = bufs.at[lax.rem(i, DEPTH)]
        for e in range(8):
            buf[:, e * 128 : (e + 1) * 128] = u[i * 8 + e, 0:SLAB, :]
        out(i).start()
        return carry

    lax.fori_loop(0, 8, step, 0)
    for n in range(3, 7):
        out_down(n).wait()
    for n in range(4, 8):
        out(n).wait()
    gate.wait()


def join(g, u, d):
    hbm = pl.BlockSpec(memory_space=pl.ANY)
    vmem = pl.BlockSpec(memory_space=pltpu.VMEM)
    dma = pltpu.SemaphoreType.DMA
    return pl.pallas_call(
        join_kernel,
        out_shape=[jax.ShapeDtypeStruct((SLAB, N * 128), BF)] * 2
        + [jax.ShapeDtypeStruct((64, N * DROWS), BF)],
        in_specs=[vmem] * 3,
        out_specs=[hbm] * 3,
        scratch_shapes=[
            pltpu.VMEM((DEPTH, SLAB, LANES), BF), pltpu.VMEM((DEPTH, 64, TILES * 128), BF),
            dma, dma((DEPTH,)), dma((DEPTH,)),
        ],
        compiler_params=pltpu.CompilerParams(vmem_limit_bytes=16 * 2**20),
        name="join",
    )(g, u.reshape(N, SLAB + 1, 128), d.reshape(N, 256, 128))


def local(wg, wu, wd, pg, qg, pu, qu, pd, qd, mg, mu, md):
    pad = jnp.zeros((15360 - COLS,), F32)
    mags = jnp.concatenate((mg, pad, mu, pad, md)).reshape(272, 128)
    g, u, d = merge(wg.T, wu.T, wd, qg, qu, qd, pg, pu, pd.T, mags)
    return tuple(o.T for o in join(g, u, d))


def solution(mesh):
    placed = (
        P("row", "col"),
        P("row", "col"),
        P("row", "col"),
        P(("row", "col"), None),
        P(None, "col"),
        P(("row", "col"), None),
        P(None, "col"),
        P(("row", "col"), None),
        P(None, "col"),
        P("col"),
        P("col"),
        P("col"),
    )
    return jax.shard_map(
        local,
        mesh=mesh,
        in_specs=placed,
        out_specs=(P(None, ("col", "row")), P(None, ("col", "row")), P(None, ("col", "row"))),
        check_vma=False,
    )
```

time: 180 us -> 169 us (0.939)
  Pallas kernels: 177 us -> 167 us
    pallas_call x4 -> x2, Pallas kernels: 177 us -> 167 us  [the longest x1 161 us: merge(): pl.pallas_call(merge_kernel, out_shape=[pltpu.VMEM(s, BF) for s in ((SLAB...]
where the time goes in v3:
time: 169 us
  Pallas kernels  167 us (99%)
    pallas_call x1, Pallas kernels, merge(): pl.pallas_call(merge_kernel, out_shape=[pltpu.VMEM(s, BF) for s in ((SLAB...  161 us
    pallas_call x1, Pallas kernels, join(): pl.pallas_call(join_kernel, out_shape=[jax.ShapeDtypeStruct((SLAB, N * 12...  5.69 us

profile of v3, /device:TPU:1, one launch (start us, length us, event | category | flops | bytes accessed | tf_op | source)
XLA Modules:
  0.0 168.8 jit_solution(15440057085428288784)
XLA Ops:
  0.6 1.6 concatenate.3
  2.2 160.8 %merge.1 = (bf16[231,8192]{1,0:T(8,128)(2,1)S(1)}, bf16[4,4,4,232,128]{4,3,2,1,0:T(8,128)(2,1)S(1)}, bf16[4,4,4,256,128]{4,3,2,1,0:T(8,128)(2,1)S(1)}, bf16[4,4,...) custom-call(bf16[14784,128]{1,0:T(8,128)(2,1)} %bitcast.11, bf16[14784,128]{1,0:T(8,128)(2,1)} %bitcast.12, ...), custom_call_target="tpu_custom_call" | custom-call | tf_op jit(solution)/shard_map/merge/pallas_call | solution.py:458
  163.1 5.7 %join.1 = (bf16[231,8192]{1,0:T(8,128)(2,1)}, bf16[231,8192]{1,0:T(8,128)(2,1)}, bf16[64,29568]{1,0:T(8,128)(2,1)}) custom-call(bf16[231,8192]{1,0:T(8,128)(2,1)S(1)} %get-tuple-element.9.g, bf16[64,232,128]{2,1,0:T(8,128)(2,1)S(1)} %bitcast.10, bf16[64,256,128]{2,1,0:T(8,128)(2,1)S(1)} %bitcast.9), custom_call_target="tpu_custom_call" | custom-call | tf_op jit(solution)/shard_map/join/pallas_call | solution.py:555
  (1 shorter events, 0.0 us)

commit v4 on v3

--- a/solution.py
+++ b/solution.py
@@ -23,11 +23,7 @@
 HALF = 8 * BLK
 ORDERS = ((2, 1, 0), (1, 0, 2), (0, 2, 1))
 FIRST = (0, 120, 240)
-SUM_ROWS = (
-    None,
-    ((120, 40), (160, 40), (200, 40)),
-    ((240, 8), (248, 8), (256, 16)),
-)
+SUM_ROWS = ((120, 48), (168, 56), (224, 48))
 GROUPS = (
     (0, ((0, 48), (80, 48), (160, 48))),
     (0, ((48, 32), (128, 32), (208, 32))),
@@ -36,6 +32,7 @@
     (2, ((0, 48), (80, 48), (176, 48))),
     (2, ((48, 32), (128, 48), (224, 32))),
 )
+G_ROWS = ((0, 80), (80, 80), (160, 80))
 P_ROWS = ((0, 32), (32, 16), (48, 16))
 
 
@@ -129,25 +126,25 @@
         near.start()
         ps.append((far, near))
 
-    def sum_copy(i, ph, t, k):
+    def sum_copy(ph, t, k):
         q, _, _ = peer_of(me, ORDERS[t][ph], k)
-        rows = pl.ds(*SUM_ROWS[i][t])
+        rows = pl.ds(*SUM_ROWS[t])
         return pltpu.make_async_remote_copy(
             src_ref=sums.at[ph, rows], dst_ref=got.at[ph, k - 1, rows],
-            send_sem=r_send.at[i, ph, t, k - 1], recv_sem=r_recv.at[i, ph, t, k - 1],
+            send_sem=r_send.at[ph, t, k - 1], recv_sem=r_recv.at[ph, t, k - 1],
             device_id=(q, core), device_id_type=MESH,
         )
 
-    def send_sums(i, ph):
+    def send_sums(ph):
         for t in range(3):
             for k in (2, 1, 3):
-                sum_copy(i, ph, t, k).start()
-
-    def take_sums(i, ph):
+                sum_copy(ph, t, k).start()
+
+    def take_sums(ph):
         for t in range(3):
             for k in (2, 1, 3):
-                sum_copy(i, ph, t, k).wait_recv()
-            rows = pl.ds(*SUM_ROWS[i][t])
+                sum_copy(ph, t, k).wait_recv()
+            rows = pl.ds(*SUM_ROWS[t])
             total = sums[ph, rows, :] + got[ph, 0, rows, :] + got[ph, 1, rows, :] + got[ph, 2, rows, :]
             if ph < 2:
                 sums[ph + 1, rows, :] = total
@@ -158,6 +155,8 @@
 
     def far_copy(g, ph, t, k):
         m, thirds = GROUPS[g]
+        if m == 0 and ph == 0:
+            thirds = G_ROWS
         axis = ORDERS[t][ph]
         p, mine, other = peer_of(me, axis, k)
         return pltpu.make_async_remote_copy(
@@ -169,6 +168,8 @@
 
     def near_copy(g, ph, t):
         m, thirds = GROUPS[g]
+        if m == 0 and ph == 0:
+            thirds = G_ROWS
         axis = ORDERS[t][ph]
         _, mine, _ = peer_of(me, axis, 1)
         return pltpu.make_async_copy(
@@ -184,42 +185,45 @@
 
     def send(g, ph):
         for t in range(3):
-            if ph > 0:
+            if ph > 0 and (g, ph) != (1, 1):
                 arrive(g, ph - 1, t)
             for k in (2, 1, 3):
                 far_copy(g, ph, t, k).start()
             near_copy(g, ph, t).start()
 
-    def send_gate(g):
-        for t, rows in enumerate(GROUPS[g][1]):
-            axis = ORDERS[t][0]
-
-            def place(i, value, axis=axis):
-                ix = [lax.div(i, 4), lax.rem(i, 4)]
-                ix.insert(axis, value)
-                return ix
-
-            def src(i, value, rows=rows, place=place):
-                z, y, x = place(i, value)
-                start = window(z * 16 + y * 4 + x) + rows[0]
-                return wg.at[pl.ds(pl.multiple_of(start, 8), rows[1])]
-
-            def go(i, carry, axis=axis, rows=rows, place=place, src=src, t=t):
-                for k in (2, 1, 3):
-                    p, mine, other = peer_of(me, axis, k)
-                    pltpu.make_async_remote_copy(
-                        src_ref=src(i, other),
-                        dst_ref=s1g.at[(*place(i, mine), pl.ds(*rows))],
-                        send_sem=x_send.at[g, 0, t, k - 1], recv_sem=x_recv.at[g, 0, t, k - 1],
-                        device_id=(p, core), device_id_type=MESH,
-                    ).start()
-                _, mine, _ = peer_of(me, axis, 1)
-                pltpu.make_async_copy(
-                    src(i, mine), s1g.at[(*place(i, mine), pl.ds(*rows))], x_loc.at[g, 0, t]
-                ).start()
-                return carry
-
-            lax.fori_loop(0, 16, go, 0)
+    def send_gate():
+        sides = []
+        for axis in range(3):
+            stride = (16, 4, 1)[axis]
+            for k in (2, 1, 3):
+                p, mine, other = peer_of(me, axis, k)
+                sides.append((axis, k, p, mine, other * stride))
+            sides.append((axis, 0, None, mine, mine * stride))
+
+        def go(i, carry):
+            for e in range(4):
+                for t, rows in enumerate(G_ROWS):
+                    for axis, k, p, mine, base in sides:
+                        if axis != ORDERS[t][0]:
+                            continue
+                        ix = [i, e]
+                        ix.insert(axis, mine)
+                        others = (i * 4 + e, i * 16 + e, i * 16 + e * 4)[axis]
+                        start = pl.multiple_of(window(base + others) + rows[0], 8)
+                        src = wg.at[pl.ds(start, rows[1])]
+                        dst = s1g.at[(*ix, pl.ds(*rows))]
+                        if k == 0:
+                            pltpu.make_async_copy(src, dst, x_loc.at[0, 0, t]).start()
+                        else:
+                            pltpu.make_async_remote_copy(
+                                src_ref=src, dst_ref=dst,
+                                send_sem=x_send.at[0, 0, t, k - 1],
+                                recv_sem=x_recv.at[0, 0, t, k - 1],
+                                device_id=(p, core), device_id_type=MESH,
+                            ).start()
+            return carry
+
+        lax.fori_loop(0, 4, go, 0)
 
     def factor_copy(ph, t, k):
         axis = ORDERS[t][ph]
@@ -361,8 +365,7 @@
             sd[a, b, c + 1, e * 64 : (e + 1) * 64, :] = z[64:128, e * 128 : (e + 1) * 128]
         return carry
 
-    send_gate(0)
-    send_gate(1)
+    send_gate()
     u_loads[1].start()
     q_loads[2].start()
     d_load.start()
@@ -383,68 +386,65 @@
     square_blocks(7, blocks, True)
     pdown[0:231, :] = both_d[0].astype(F32).T
     pdown[231:462, :] = both_d[1].astype(F32).T
-    send_sums(1, 0)
-    send(0, 1)
     q_loads[2].wait()
     d_load.wait()
-    lax.fori_loop(0, 12, square_down, 0)
+    lax.fori_loop(0, DCOLS // 128, square_down, 0)
+    send_sums(0)
+    send(0, 1)
+    q_loads[3].wait()
+    take_sums(0)
+    send_sums(1)
+    send(1, 1)
     take_factor(0)
     send_factor(1)
-    q_loads[3].wait()
-    take_sums(1, 0)
-    send_sums(1, 1)
-    send(1, 1)
-    lax.fori_loop(12, DCOLS // 128, square_down, 0)
-    send_sums(2, 0)
-    take_sums(1, 1)
-    send_sums(1, 2)
+    take_sums(1)
+    send_sums(2)
     send(0, 2)
-    take_factor(1)
-    send_factor(2)
-    take_sums(1, 2)
+    take_sums(2)
     send(1, 2)
     merge_up(0)
     merge_up(1)
-    take_sums(2, 0)
-    send_sums(2, 1)
     send(2, 0)
     send(3, 0)
+    take_factor(1)
+    send_factor(2)
+    lax.fori_loop(0, DCOLS // 256, merge_down, 0)
+    send(2, 1)
+    lax.fori_loop(DCOLS // 256, DCOLS // 128, merge_down, 0)
+    send(3, 1)
+    send(4, 0)
+    send(2, 2)
+    send(5, 0)
     q_loads[0].wait()
     own_columns()
     take_factor(2)
     for t in range(3):
         arrive(0, 2, t)
         arrive(1, 2, t)
-    lax.fori_loop(0, N, gate_squares, 0)
+    send(3, 2)
+    lax.fori_loop(0, N // 2, gate_squares, 0)
+    send(4, 1)
+    lax.fori_loop(N // 2, N, gate_squares, 0)
     gate_scale()
-    take_sums(2, 1)
-    send_sums(2, 2)
-    send(2, 1)
-    lax.fori_loop(0, N, gate_finish, 0)
-    send(3, 1)
-    take_sums(2, 2)
-    lax.fori_loop(0, DCOLS // 256, merge_down, 0)
-    send(2, 2)
-    lax.fori_loop(DCOLS // 256, DCOLS // 128, merge_down, 0)
-    send(4, 0)
-    send(5, 0)
-    send(3, 2)
-    for ph in (1, 2):
-        send(4, ph)
-        send(5, ph)
+    send(5, 1)
+    lax.fori_loop(0, N // 2, gate_finish, 0)
+    send(4, 2)
+    lax.fori_loop(N // 2, N, gate_finish, 0)
+    send(5, 2)
     for g in range(2, 6):
         for t in range(3):
             arrive(g, 2, t)
     for g in range(6):
         for ph in range(3):
+            if (g, ph) == (1, 0):
+                continue
             for t in range(3):
                 for k in (1, 2, 3):
                     far_copy(g, ph, t, k).wait_send()
     for ph in range(3):
         for t in range(3):
             for k in (1, 2, 3):
-                sum_copy(1, ph, t, k).wait_send()
-                sum_copy(2, ph, t, k).wait_send()
+                sum_copy(ph, t, k).wait_send()
                 factor_copy(ph, t, k).wait_send()
 
 
@@ -475,7 +475,7 @@
             pltpu.VMEM((WIDE, RANK), BF), pltpu.VMEM((384, 128), F32),
             pltpu.VMEM((WIDE, 128), F32), pltpu.VMEM((WIDE + 8, 128), F32),
             dma((3,)), dma((4,)), dma((3,)), dma((3,)), dma((3,)),
-            dma((3, 3, 3, 3)), dma((3, 3, 3, 3)),
+            dma((3, 3, 3)), dma((3, 3, 3)),
             dma((6, 3, 3, 3)), dma((6, 3, 3, 3)), dma((6, 3, 3)),
             dma((3, 3, 3)), dma((3, 3, 3)),
         ],

time: 169 us -> 162 us (0.959)
  Pallas kernels: 167 us -> 159 us
    pallas_call x1, Pallas kernels: 161 us -> 154 us  [merge(): pl.pallas_call(merge_kernel, out_shape=[pltpu.VMEM(s, BF) for s in ((SLAB...]
where the time goes in v4:
time: 162 us; the launch traced here: 161 us
  Pallas kernels  159 us (98%)
    pallas_call x1, Pallas kernels, merge(): pl.pallas_call(merge_kernel, out_shape=[pltpu.VMEM(s, BF) for s in ((SLAB...  154 us
    pallas_call x1, Pallas kernels, join(): pl.pallas_call(join_kernel, out_shape=[jax.ShapeDtypeStruct((SLAB, N * 12...  5.69 us

profile of v4, /device:TPU:1, one launch (start us, length us, event | category | flops | bytes accessed | tf_op | source)
XLA Modules:
  0.0 161.4 jit_solution(6393622349579840591)
XLA Ops:
  0.6 1.6 concatenate.3
  2.2 153.5 %merge.1 = (bf16[231,8192]{1,0:T(8,128)(2,1)S(1)}, bf16[4,4,4,232,128]{4,3,2,1,0:T(8,128)(2,1)S(1)}, bf16[4,4,4,256,128]{4,3,2,1,0:T(8,128)(2,1)S(1)}, bf16[4,4,...) custom-call(bf16[14784,128]{1,0:T(8,128)(2,1)} %bitcast.11, bf16[14784,128]{1,0:T(8,128)(2,1)} %bitcast.12, ...), custom_call_target="tpu_custom_call" | custom-call | tf_op jit(solution)/shard_map/merge/pallas_call | solution.py:458
  155.8 5.7 %join.1 = (bf16[231,8192]{1,0:T(8,128)(2,1)}, bf16[231,8192]{1,0:T(8,128)(2,1)}, bf16[64,29568]{1,0:T(8,128)(2,1)}) custom-call(bf16[231,8192]{1,0:T(8,128)(2,1)S(1)} %get-tuple-element.9.g, bf16[64,232,128]{2,1,0:T(8,128)(2,1)S(1)} %bitcast.10, bf16[64,256,128]{2,1,0:T(8,128)(2,1)S(1)} %bitcast.9), custom_call_target="tpu_custom_call" | custom-call | tf_op jit(solution)/shard_map/join/pallas_call | solution.py:555
  (1 shorter events, 0.0 us)

commit v5 on v4

--- a/solution.py
+++ b/solution.py
@@ -33,7 +33,7 @@
     (2, ((48, 32), (128, 48), (224, 32))),
 )
 G_ROWS = ((0, 80), (80, 80), (160, 80))
-P_ROWS = ((0, 32), (32, 16), (48, 16))
+P_ROWS = ((0, 16), (16, 16))
 
 
 def peer_of(me, axis, k):
@@ -91,7 +91,7 @@
 
 
 def merge_kernel(
-    wg, wu, wd, qg, qu, qd, pg, pu, pd, mags,
+    wg, wu, wd, qg, qu, qd, pg, pu, pd, mg, mu, md,
     og, ou, od, s1u, s1d,
     vu, vd, rg, ru, rd, su, sd, s1g, s2g, s3g, s2u, s2d,
     full, turn, both_g, both_u, both_d, pdown, mag, sums, got, scale,
@@ -110,7 +110,7 @@
     d_load = pltpu.make_async_copy(wd, vd, w_sem.at[2])
     q_loads = [
         pltpu.make_async_copy(src, dst, q_sem.at[i])
-        for i, (src, dst) in enumerate(((qg, rg), (qu, ru), (qd, rd), (mags, mag)))
+        for i, (src, dst) in enumerate(((qg, rg), (qu, ru), (qd, rd)))
     ]
     q_loads[1].start()
     u_loads[0].start()
@@ -225,13 +225,16 @@
 
         lax.fori_loop(0, 4, go, 0)
 
+    my_half = pl.multiple_of(core * 32, 32)
+
     def factor_copy(ph, t, k):
         axis = ORDERS[t][ph]
         p, _, _ = peer_of(me, axis, k)
         ix = list(mine_at)
         for done in ORDERS[t][:ph]:
             ix[done] = slice(None)
-        block = gathered.at[(*ix, pl.ds(*P_ROWS[t]))]
+        first, rows = P_ROWS[t]
+        block = gathered.at[(*ix, pl.ds(pl.multiple_of(my_half + first, 16), rows))]
         return pltpu.make_async_remote_copy(
             src_ref=block, dst_ref=block,
             send_sem=g_send.at[ph, t, k - 1], recv_sem=g_recv.at[ph, t, k - 1],
@@ -239,14 +242,21 @@
         )
 
     def send_factor(ph):
-        for t in range(3):
+        for t in range(2):
             for k in (2, 1, 3):
                 factor_copy(ph, t, k).start()
 
     def take_factor(ph):
-        for t in range(3):
+        for t in range(2):
             for k in (2, 1, 3):
                 factor_copy(ph, t, k).wait_recv()
+
+    def swap_factor():
+        block = gathered.at[:, :, :, pl.ds(my_half, 32)]
+        return pltpu.make_async_remote_copy(
+            src_ref=block, dst_ref=block, send_sem=p_send.at[3], recv_sem=p_recv.at[3],
+            device_id=(me, 1 - core), device_id_type=MESH,
+        )
 
     def source(i):
         return lax.div(i, 16), lax.rem(lax.div(i, 4), 4), lax.rem(i, 4)
@@ -369,7 +379,6 @@
     u_loads[1].start()
     q_loads[2].start()
     d_load.start()
-    q_loads[3].start()
     q_loads[0].start()
     for far, near in ps:
         near.wait()
@@ -377,7 +386,8 @@
     turn[...] = jnp.zeros_like(turn)
     acc[...] = jnp.zeros_like(acc)
     qwin[...] = jnp.zeros_like(qwin)
-    gathered[mine_at] = both_g[...].reshape(2 * RANK, RANK).astype(F32).T.astype(BF)
+    shift[0:RANK, :] = both_g[...].reshape(2 * RANK, RANK).astype(F32).T
+    gathered[(*mine_at, pl.ds(my_half, 32))] = shift[pl.ds(my_half, 32), :].astype(BF)
     q_loads[1].wait()
     u_loads[0].wait()
     square_blocks(0, 7, False)
@@ -391,7 +401,17 @@
     lax.fori_loop(0, DCOLS // 128, square_down, 0)
     send_sums(0)
     send(0, 1)
-    q_loads[3].wait()
+    mag[...] = jnp.zeros_like(mag)
+    mag[FIRST[2] : FIRST[2] + 32, :] = md[...]
+    for top, src in ((FIRST[0], mg), (FIRST[1], mu)):
+
+        def rows(j, carry, top=top, src=src):
+            at_lane = pl.multiple_of(j * 128, 128)
+            mag[pl.ds(top + j, 1), :] = src[pl.ds(at_lane, 128)].reshape(1, 128)
+            return carry
+
+        lax.fori_loop(0, COLS // 128, rows, 0)
+        mag[top + 115 : top + 116, 0:64] = src[COLS - 64 : COLS].reshape(1, 64)
     take_sums(0)
     send_sums(1)
     send(1, 1)
@@ -418,10 +438,12 @@
     q_loads[0].wait()
     own_columns()
     take_factor(2)
+    swap_factor().start()
     for t in range(3):
         arrive(0, 2, t)
         arrive(1, 2, t)
     send(3, 2)
+    swap_factor().wait()
     lax.fori_loop(0, N // 2, gate_squares, 0)
     send(4, 1)
     lax.fori_loop(N // 2, N, gate_squares, 0)
@@ -445,10 +467,11 @@
         for t in range(3):
             for k in (1, 2, 3):
                 sum_copy(ph, t, k).wait_send()
-                factor_copy(ph, t, k).wait_send()
-
-
-def merge(wg, wu, wd, qg, qu, qd, pg, pu, pd, mags):
+                if t < 2:
+                    factor_copy(ph, t, k).wait_send()
+
+
+def merge(wg, wu, wd, qg, qu, qd, pg, pu, pd, mg, mu, md):
     hbm = pl.BlockSpec(memory_space=pl.ANY)
     vmem = pl.BlockSpec(memory_space=pltpu.VMEM)
     wide = (4, 4, 4, WIDE, 128)
@@ -459,7 +482,7 @@
         merge_kernel,
         out_shape=[pltpu.VMEM(s, BF) for s in ((SLAB, N * 128), slab, dslab)]
         + [jax.ShapeDtypeStruct(s, BF) for s in (slab, dslab)],
-        in_specs=[hbm] * 6 + [vmem] * 3 + [hbm],
+        in_specs=[hbm] * 6 + [vmem] * 6,
         out_specs=[vmem] * 3 + [hbm] * 2,
         scratch_shapes=[
             pltpu.VMEM((COLS, 128), BF), pltpu.VMEM((DROWS, DCOLS), BF),
@@ -474,16 +497,16 @@
             pltpu.VMEM((4, 4, 4, RANK, 128), BF), pltpu.VMEM((384, RANK), F32),
             pltpu.VMEM((WIDE, RANK), BF), pltpu.VMEM((384, 128), F32),
             pltpu.VMEM((WIDE, 128), F32), pltpu.VMEM((WIDE + 8, 128), F32),
-            dma((3,)), dma((4,)), dma((3,)), dma((3,)), dma((3,)),
+            dma((3,)), dma((4,)), dma((4,)), dma((4,)), dma((3,)),
             dma((3, 3, 3)), dma((3, 3, 3)),
             dma((6, 3, 3, 3)), dma((6, 3, 3, 3)), dma((6, 3, 3)),
-            dma((3, 3, 3)), dma((3, 3, 3)),
+            dma((3, 2, 3)), dma((3, 2, 3)),
         ],
         compiler_params=pltpu.CompilerParams(
             collective_id=0, has_side_effects=True, vmem_limit_bytes=54 * 10**6
         ),
         name="merge",
-    )(wg, wu, wd, qg, qu, qd, pg, pu, pd, mags)[:3]
+    )(wg, wu, wd, qg, qu, qd, pg, pu, pd, mg, mu, md)[:3]
 
 
 LANES = 1024
@@ -568,9 +591,7 @@
 
 
 def local(wg, wu, wd, pg, qg, pu, qu, pd, qd, mg, mu, md):
-    pad = jnp.zeros((15360 - COLS,), F32)
-    mags = jnp.concatenate((mg, pad, mu, pad, md)).reshape(272, 128)
-    g, u, d = merge(wg.T, wu.T, wd, qg, qu, qd, pg, pu, pd.T, mags)
+    g, u, d = merge(wg.T, wu.T, wd, qg, qu, qd, pg, pu, pd.T, mg, mu, md.reshape(32, 128))
     return tuple(o.T for o in join(g, u, d))
 
 

time: 162 us -> 157 us (0.969)
  Pallas kernels: 159 us -> 156 us
    pallas_call x1, Pallas kernels: 154 us -> 151 us  [merge(): pl.pallas_call(merge_kernel, out_shape=[pltpu.VMEM(s, BF) for s in ((SLAB...]
where the time goes in v5:
time: 157 us
  Pallas kernels  156 us (99%)
    pallas_call x1, Pallas kernels, merge(): pl.pallas_call(merge_kernel, out_shape=[pltpu.VMEM(s, BF) for s in ((SLAB...  151 us
    pallas_call x1, Pallas kernels, join(): pl.pallas_call(join_kernel, out_shape=[jax.ShapeDtypeStruct((SLAB, N * 12...  5.69 us

profile of v5, /device:TPU:1, one launch (start us, length us, event | category | flops | bytes accessed | tf_op | source)
XLA Modules:
  0.0 157.0 jit_solution(5974306241435155213)
XLA Ops:
  0.6 150.7 %merge.1 = (bf16[231,8192]{1,0:T(8,128)(2,1)S(1)}, bf16[4,4,4,232,128]{4,3,2,1,0:T(8,128)(2,1)S(1)}, bf16[4,4,4,256,128]{4,3,2,1,0:T(8,128)(2,1)S(1)}, bf16[4,4,...) custom-call(bf16[14784,128]{1,0:T(8,128)(2,1)} %bitcast.11, bf16[14784,128]{1,0:T(8,128)(2,1)} %bitcast.12, ...), custom_call_target="tpu_custom_call" | custom-call | tf_op jit(solution)/shard_map/merge/pallas_call | solution.py:481
  151.3 5.7 %join.1 = (bf16[231,8192]{1,0:T(8,128)(2,1)}, bf16[231,8192]{1,0:T(8,128)(2,1)}, bf16[64,29568]{1,0:T(8,128)(2,1)}) custom-call(bf16[231,8192]{1,0:T(8,128)(2,1)S(1)} %get-tuple-element.9.g, bf16[64,232,128]{2,1,0:T(8,128)(2,1)S(1)} %bitcast.10, bf16[64,256,128]{2,1,0:T(8,128)(2,1)S(1)} %bitcast.9), custom_call_target="tpu_custom_call" | custom-call | tf_op jit(solution)/shard_map/join/pallas_call | solution.py:578

commit v6 on v5

--- a/solution.py
+++ b/solution.py
@@ -435,6 +435,7 @@
     send(4, 0)
     send(2, 2)
     send(5, 0)
+    send(3, 2)
     q_loads[0].wait()
     own_columns()
     take_factor(2)
@@ -442,7 +443,6 @@
     for t in range(3):
         arrive(0, 2, t)
         arrive(1, 2, t)
-    send(3, 2)
     swap_factor().wait()
     lax.fori_loop(0, N // 2, gate_squares, 0)
     send(4, 1)

time: 157 us -> 157 us (level)
  no operation moved by 1% of the time
where the time goes in v6:
time: 157 us
  Pallas kernels  156 us (99%)
    pallas_call x1, Pallas kernels, merge(): pl.pallas_call(merge_kernel, out_shape=[pltpu.VMEM(s, BF) for s in ((SLAB...  151 us
    pallas_call x1, Pallas kernels, join(): pl.pallas_call(join_kernel, out_shape=[jax.ShapeDtypeStruct((SLAB, N * 12...  5.69 us

profile of v6, /device:TPU:1, one launch (start us, length us, event | category | flops | bytes accessed | tf_op | source)
XLA Modules:
  0.0 157.0 jit_solution(14799811784607026066)
XLA Ops:
  0.6 150.7 %merge.1 = (bf16[231,8192]{1,0:T(8,128)(2,1)S(1)}, bf16[4,4,4,232,128]{4,3,2,1,0:T(8,128)(2,1)S(1)}, bf16[4,4,4,256,128]{4,3,2,1,0:T(8,128)(2,1)S(1)}, bf16[4,4,...) custom-call(bf16[14784,128]{1,0:T(8,128)(2,1)} %bitcast.11, bf16[14784,128]{1,0:T(8,128)(2,1)} %bitcast.12, ...), custom_call_target="tpu_custom_call" | custom-call | tf_op jit(solution)/shard_map/merge/pallas_call | solution.py:481
  151.3 5.7 %join.1 = (bf16[231,8192]{1,0:T(8,128)(2,1)}, bf16[231,8192]{1,0:T(8,128)(2,1)}, bf16[64,29568]{1,0:T(8,128)(2,1)}) custom-call(bf16[231,8192]{1,0:T(8,128)(2,1)S(1)} %get-tuple-element.9.g, bf16[64,232,128]{2,1,0:T(8,128)(2,1)S(1)} %bitcast.10, bf16[64,256,128]{2,1,0:T(8,128)(2,1)S(1)} %bitcast.9), custom_call_target="tpu_custom_call" | custom-call | tf_op jit(solution)/shard_map/join/pallas_call | solution.py:578
